TPU v7x, 512 devices: a whole 4x4x16 slice. The times are simulated.
512 devices in a mesh: dp: 64 (over y, z_lo, core), space: 8 (over x, z_hi).
Axes of the slice: x: 4, y: 4, z: 16 (z_hi: 2, z_lo: 8; z = z_hi * 8 + z_lo), core: 2. Of those that a mesh axis runs over, the one named last changes fastest.
Arguments:
- volume: float32 [64, 32, 32, 256], P('dp', None, 'space'), may hold values from -6 to 6
- cotangent: float32 [64, 64, 128], P('dp', 'space'), may hold values from -6 to 6
- w_first: float32 [64, 2048], replicated, may hold values from -0.125 to 0.125
- b_first: float32 [64], replicated, may hold values from -3 to 3
- w_second: float32 [64, 4096], P('space'), may hold values from -0.09375 to 0.09375
- b_second: float32 [64], P('space'), may hold values from -3 to 3
Outputs:
- output: float32 [64, 64, 128], P('dp', 'space')
- grad_volume: float32 [64, 32, 32, 256], P('dp', None, 'space')
- grad_w_first: float32 [64, 2048], replicated
- grad_b_first: float32 [64], replicated
- grad_w_second: float32 [64, 4096], P('space')
- grad_b_second: float32 [64], P('space')
All inputs are finite; a program needn't handle non-finite values.
Results may differ from a plain program's by a relative error of at most 0.00018.
Values sent between devices are 32-bit elements; how exact they have to be, the bound alone decides.
A program may use at most 128 MiB of HBM per device.

v0:
```python
import jax
import jax.numpy as jnp
from jax import lax
from jax.sharding import PartitionSpec as P

HEIGHT = 16
WIDTH = 16


SLOPE = 0.3
PRECISE = lax.Precision.HIGHEST


def padded_2(cells, sides, width):
    for axis, dim in sides:
        count = lax.axis_size(axis)
        ends = count - 1
        head = lax.slice_in_dim(cells, 0, width, axis=dim)
        tail = lax.slice_in_dim(cells, cells.shape[dim] - width, cells.shape[dim], axis=dim)
        cells = jnp.concatenate(
            [
                lax.ppermute(tail, axis, [(i, (i + 1) % count) for i in range(ends)]),
                cells,
                lax.ppermute(head, axis, [((i + 1) % count, i) for i in range(ends)]),
            ],
            axis=dim,
        )
    return cells


def activate(pre_value):
    return SLOPE * pre_value + (1.0 - SLOPE) * jax.nn.softplus(pre_value)


def slope_of(pre_value):
    return SLOPE + (1.0 - SLOPE) * jax.nn.sigmoid(pre_value)


def offsets(out_height, out_width):
    plane_size = (out_height + 1) * (out_width + 1)
    return [
        (a, b, c, a * plane_size + b * (out_width + 1) + c)
        for a in range(2)
        for b in range(2)
        for c in range(2)
    ]


def to_blocks(padded):
    sample_count, channels, grid_depth, grid_height, grid_width = padded.shape
    split_grid = padded.reshape(
        sample_count, channels, grid_depth // 2, 2, grid_height // 2, 2, grid_width // 2, 2
    )
    split_grid = split_grid.transpose(0, 1, 3, 5, 7, 2, 4, 6)
    return split_grid.reshape(
        sample_count, channels * 8, grid_depth // 2 * (grid_height // 2) * (grid_width // 2)
    )


def from_blocks(flat_grid, channels, block_depth, block_height, block_width):
    sample_count = flat_grid.shape[0]
    split_grid = flat_grid.reshape(
        sample_count, channels, 2, 2, 2, block_depth, block_height, block_width
    )
    split_grid = split_grid.transpose(0, 1, 5, 2, 6, 3, 7, 4)
    return split_grid.reshape(
        sample_count, channels, 2 * block_depth, 2 * block_height, 2 * block_width
    )


def tap_weight(weight, channels, a, b, c):
    out_count = weight.shape[0]
    weight_parts = weight.reshape(out_count, channels, 2, 2, 2, 2, 2, 2)
    return weight_parts[:, :, a, :, b, :, c, :].reshape(out_count, channels * 8)


def pad_planes(field, plane_height, plane_width):
    sample_count, channels, depth_rows = field.shape[:3]
    field_grid = field.reshape(sample_count, channels, depth_rows, plane_height, plane_width)
    return jnp.pad(field_grid, ((0, 0), (0, 0), (0, 0), (1, 1), (1, 1)))


def conv_forward(padded, weight, bias_vector):
    sample_count, channels, grid_depth, grid_height, grid_width = padded.shape
    out_depth, out_height, out_width = (
        grid_depth // 2 - 1,
        grid_height // 2 - 1,
        grid_width // 2 - 1,
    )
    blocks = to_blocks(padded)
    length = out_depth * (out_height + 1) * (out_width + 1)
    blocks = jnp.pad(blocks, ((0, 0), (0, 0), (0, out_width + 2)))
    running = jnp.zeros((sample_count, weight.shape[0], length), jnp.float32)
    for a, b, c, offset_at in offsets(out_height, out_width):
        window = lax.slice_in_dim(blocks, offset_at, offset_at + length, axis=2)
        running = running + jnp.einsum(
            "ok,skt->sot", tap_weight(weight, channels, a, b, c), window, precision=PRECISE
        )
    field_grid = running.reshape(sample_count, -1, out_depth, out_height + 1, out_width + 1)[
        :, :, :, :out_height, :out_width
    ]
    pre_value = (
        field_grid.reshape(sample_count, -1, out_depth * out_height * out_width)
        + bias_vector[None, :, None]
    )
    return (pre_value, blocks)


def extend_rows(gradient, out_depth, out_height, out_width):
    sample_count, out_count = gradient.shape[:2]
    field_grid = gradient.reshape(sample_count, out_count, out_depth, out_height, out_width)
    field_grid = jnp.pad(field_grid, ((0, 0), (0, 0), (0, 0), (0, 1), (0, 1)))
    return field_grid.reshape(
        sample_count, out_count, out_depth * (out_height + 1) * (out_width + 1)
    )


def weight_grad(blocks, grad_ext, channels, out_height, out_width):
    length = grad_ext.shape[2]
    out_count = grad_ext.shape[1]
    pieces = []
    for a, b, c, offset_at in offsets(out_height, out_width):
        window = lax.slice_in_dim(blocks, offset_at, offset_at + length, axis=2)
        pieces.append(jnp.einsum("sot,skt->ok", grad_ext, window, precision=PRECISE))
    stacked = jnp.stack(pieces).reshape(2, 2, 2, out_count, channels, 2, 2, 2)
    return stacked.transpose(3, 4, 0, 5, 1, 6, 2, 7).reshape(out_count, channels * 64)


def input_grad(grad_ext, weight, channels, out_depth, out_height, out_width):
    plane_size = (out_height + 1) * (out_width + 1)
    full_length = (out_depth + 1) * plane_size
    length = grad_ext.shape[2]
    lead_pad = plane_size + out_width + 2
    padded = jnp.pad(grad_ext, ((0, 0), (0, 0), (lead_pad, full_length - length)))
    running = jnp.zeros((grad_ext.shape[0], channels * 8, full_length), jnp.float32)
    for a, b, c, offset_at in offsets(out_height, out_width):
        window = lax.slice_in_dim(
            padded, lead_pad - offset_at, lead_pad - offset_at + full_length, axis=2
        )
        running = running + jnp.einsum(
            "ok,sot->skt", tap_weight(weight, channels, a, b, c), window, precision=PRECISE
        )
    return from_blocks(running, channels, out_depth + 1, out_height + 1, out_width + 1)


def on_device(volume, cotangent, w_first, b_first, w_second, b_second):
    sample_count, in_channels, slab_rows = volume.shape[:3]
    mid_channels = w_first.shape[0]
    sample_scale = 1.0 / (sample_count * lax.axis_size("dp"))
    mid_rows, mid_height, mid_width = (slab_rows // 2, HEIGHT // 2, WIDTH // 2)
    out_height, out_width = (HEIGHT // 4, WIDTH // 4)
    volume_rims = padded_2(volume, (("space", 2),), 1)
    pre_first, blocks_first = conv_forward(pad_planes(volume_rims, HEIGHT, WIDTH), w_first, b_first)
    layered = activate(pre_first).reshape(
        sample_count, mid_channels, mid_rows, mid_height * mid_width
    )
    full_middle = lax.all_gather(layered, "space", axis=2, tiled=True)
    depth_total = full_middle.shape[2]
    out_depth = depth_total // 2
    middle_padded = jnp.pad(full_middle, ((0, 0), (0, 0), (1, 1), (0, 0)))
    pre_second, blocks_second = conv_forward(
        pad_planes(middle_padded, mid_height, mid_width), w_second, b_second
    )
    output = activate(pre_second)
    grad_second = cotangent * slope_of(pre_second)
    grad_ext = extend_rows(grad_second, out_depth, out_height, out_width)
    part_weight = (
        weight_grad(blocks_second, grad_ext, mid_channels, out_height, out_width) * sample_scale
    )
    part_bias = jnp.sum(grad_second, axis=(0, 2)) * sample_scale
    grad_w_second, grad_b_second = lax.psum((part_weight, part_bias), "dp")
    grad_padded = input_grad(grad_ext, w_second, mid_channels, out_depth, out_height, out_width)
    grad_full = grad_padded[:, :, 1 : 1 + depth_total, 1 : 1 + mid_height, 1 : 1 + mid_width]
    grad_full = grad_full.reshape(sample_count, mid_channels, depth_total, mid_height * mid_width)
    grad_middle = lax.psum_scatter(grad_full, "space", scatter_dimension=2, tiled=True)
    grad_first = grad_middle.reshape(sample_count, mid_channels, -1) * slope_of(pre_first)
    first_ext = extend_rows(grad_first, mid_rows, mid_height, mid_width)
    part_first = (
        weight_grad(blocks_first, first_ext, in_channels, mid_height, mid_width) * sample_scale
    )
    part_first_bias = jnp.sum(grad_first, axis=(0, 2)) * sample_scale
    grad_w_first, grad_b_first = lax.psum((part_first, part_first_bias), ("dp", "space"))
    first_layered = grad_first.reshape(sample_count, mid_channels, mid_rows, mid_height * mid_width)
    first_rims = padded_2(first_layered, (("space", 2),), 1)
    rims_first = extend_rows(
        first_rims.reshape(sample_count, mid_channels, -1), mid_rows + 2, mid_height, mid_width
    )
    grad_input = input_grad(rims_first, w_first, in_channels, mid_rows + 2, mid_height, mid_width)
    grad_volume = grad_input[:, :, 3 : 3 + slab_rows, 1 : 1 + HEIGHT, 1 : 1 + WIDTH]
    grad_volume = grad_volume.reshape(sample_count, in_channels, slab_rows, HEIGHT * WIDTH)
    return (output, grad_volume, grad_w_first, grad_b_first, grad_w_second, grad_b_second)


def solution(mesh):
    in_specs = (
        P("dp", None, "space", None),
        P("dp", "space", None),
        P(),
        P(),
        P("space", None),
        P("space"),
    )
    out_specs = (
        P("dp", "space", None),
        P("dp", None, "space", None),
        P(),
        P(),
        P("space", None),
        P("space"),
    )
    return jax.shard_map(
        on_device, mesh=mesh, in_specs=in_specs, out_specs=out_specs, check_vma=False
    )
```

profile of v0, /device:TPU:1, one launch (start us, length us, event | category | flops | bytes accessed | tf_op | source)
XLA Modules:
  0.0 1513.3 jit_solution(13303179598115866519)
XLA Ops:
  10.0 16.9 %collective-permute-start = (f32[1,32,1,256]{1,3,2,0:T(8,128)}, f32[1,32,1,256]{1,3,2,0:T(8,128)}, u32[]{:S(2)}, u32[]{:S(2)}) collective-permute-start(f32[1,32,1,256]{1,3,2,0:T(8,128)} %get-tuple-element.56), channel_id=1, source_target_pairs={{0,1},{1,2},{2,3},{3,4},{4,5},{5,6},{6,7},{8,9},{9,10},{10,11},{11... | collective-permute-start | bytes 98312 | tf_op jit(solution)/shard_map/ppermute | solution.py:22
  26.9 1.3 collective-permute-start.1
  28.2 1.4 copy.165
  30.2 1.8 fusion.94
  33.1 14.2 collective-permute-done.1
  49.4 6.5 copy.164
  56.0 4.2 reshape.552
  64.8 75.4 %all_gather.3 = f32[1,64,16,64]{3,1,0,2:T(8,128)S(1)} all-gather(f32[1,64,2,64]{3,1,0,2:T(8,128)S(1)} %copy.168), channel_id=1, replica_groups=mesh['dp'=64,'space'=8] {'space'}, dimensions={2}, use_global_device_ids=true | all-gather | bytes 294912 | tf_op jit(solution)/shard_map/all_gather | solution.py:157
  141.6 15.9 %copy.170 = f32[1,64,2,2,2,9,5,5]{7,6,5,4,3,2,1,0:T(8,128)} copy(f32[1,64,2,2,2,9,5,5]{1,0,4,7,3,6,2,5:T(1,128)S(1)} %bitcast.316) | data formatting | bytes 921600 | tf_op jit(solution)/shard_map/transpose | solution.py:54
  157.5 10.5 reshape.566
  174.0 1.3 fusion.92
  182.4 1.5 copy.197
  183.9 2.6 copy.198
  187.4 1.2 pad_slice_fusion
  189.2 1.6 copy.176
  190.8 1.6 copy.177
  193.6 1.3 convolution_add_fusion.6
  194.9 1.3 convolution_add_fusion.5
  199.5 8.4 reshape.588
  207.8 11.7 copy.184
  220.4 214.3 %psum.31 = f32[8]{0:T(128)} all-reduce(f32[8]{0:T(128)S(1)} %broadcast_multiply_fusion.2), channel_id=1, replica_groups=mesh['dp'=64,'space'=8] {'dp'}, use_global_device_ids=true, to_apply=%region_6.7 | all-reduce | flops 8 | bytes 64 | tf_op jit(solution)/shard_map/psum | solution.py:171
  434.8 592.7 %all-reduce.15.cloned.1.call-done = f32[8,4096]{0,1:T(8,128)} async-done(((f32[8,4096]{0,1:T(8,128)}), f32[8,4096]{0,1:T(8,128)}) %all-reduce.15.cloned.1.call-update) | async-done | bytes 131088 | tf_op jit(solution)/shard_map/psum | solution.py:171
  1027.5 2.8 copy.201
  1035.4 1.6 copy.196
  1037.1 4.8 collective-permute-start.2
  1041.9 1.3 collective-permute-start.3
  1043.2 113.0 %psum.29 = f32[64]{0:T(128)} all-reduce(f32[64]{0:T(128)S(1)} %broadcast_multiply_fusion.3), channel_id=1, replica_groups=mesh['dp'=64,'space'=8] {'dp','space'}, use_global_device_ids=true, to_apply=%region_3.4 | all-reduce | flops 64 | bytes 512 | tf_op jit(solution)/shard_map/psum | solution.py:182
  1156.5 4.0 pad_slice_fusion.8
  1166.3 5.5 reshape.600
  1171.8 7.9 copy.194
  1180.6 322.7 %all-reduce.13.cloned.1.call-done = f32[64,2048]{0,1:T(8,128)} async-done(((f32[64,2048]{0,1:T(8,128)}), f32[64,2048]{0,1:T(8,128)}) %all-reduce.13.cloned.1.call-update) | async-done | bytes 524304 | tf_op jit(solution)/shard_map/psum | solution.py:182
  1503.4 2.3 copy.200
  (183 shorter events, 43.2 us)
Async XLA Ops:
  8.0 21.6 %copy-start.31 = (f32[8,4096]{1,0:T(8,128)S(1)}, f32[8,4096]{1,0:T(8,128)}, u32[]{:S(2)}) copy-start(f32[8,4096]{1,0:T(8,128)} %param.10) | copy-start | bytes 393220
  8.0 1019.5 %all-reduce.15.cloned.1.call-start = ((), (), s32[]{:S(2)}) async-start(), calls=%async_computation.3 | async-start | bytes 4194304 | tf_op jit(solution)/shard_map/psum | solution.py:171
  9.2 19.0 %copy-start = (f32[1,32,4,256]{1,3,2,0:T(8,128)}, f32[1,32,4,256]{1,3,2,0:T(8,128)S(1)}, u32[]{:S(2)}) copy-start(f32[1,32,4,256]{1,3,2,0:T(8,128)S(1)} %copy.161) | copy-start | bytes 393220
  10.0 23.1 %collective-permute-start = (f32[1,32,1,256]{1,3,2,0:T(8,128)}, f32[1,32,1,256]{1,3,2,0:T(8,128)}, u32[]{:S(2)}, u32[]{:S(2)}) collective-permute-start(f32[1,32,1,256]{1,3,2,0:T(8,128)} %get-tuple-element.56), channel_id=1, source_target_pairs={{0,1},{1,2},{2,3},{3,4},{4,5},{5,6},{6,7},{8,9},{9,10},{10,11},{11... | collective-permute-start | bytes 98312 | tf_op jit(solution)/shard_map/ppermute | solution.py:22
  26.9 20.4 %collective-permute-start.1 = (f32[1,32,1,256]{1,3,2,0:T(8,128)}, f32[1,32,1,256]{1,3,2,0:T(8,128)}, u32[]{:S(2)}, u32[]{:S(2)}) collective-permute-start(f32[1,32,1,256]{1,3,2,0:T(8,128)} %get-tuple-element.57), channel_id=1, source_target_pairs={{1,0},{2,1},{3,2},{4,3},{5,4},{6,5},{7,6},{9,8},{10,9},{11,10},{12... | collective-permute-start | bytes 98312 | tf_op jit(solution)/shard_map/ppermute | solution.py:24
  31.9 15.3 %copy-start.1 = (f32[1,32,4,256]{1,3,2,0:T(8,128)S(1)}, f32[1,32,4,256]{1,3,2,0:T(8,128)}, u32[]{:S(2)}) copy-start(f32[1,32,4,256]{1,3,2,0:T(8,128)} %copy-done) | copy-start | bytes 393220
  56.0 4.3 copy-start.25
  56.0 4.7 copy-start.23
  56.0 5.2 copy-start.21
  56.0 5.6 copy-start.19
  60.2 2.8 copy-start.13
  60.6 3.5 copy-start.32
  157.5 10.5 copy-start.11
  157.5 11.1 copy-start.9
  157.5 11.8 copy-start.7
  168.0 2.8 copy-start.4
  168.0 3.5 copy-start.3
  168.6 3.7 copy-start.2
  170.1 3.9 copy-start.34
  170.1 3.9 copy-start.35
  186.5 7.1 copy-start.10
  186.5 8.4 copy-start.8
  186.5 843.8 %reduce-scatter.2.cloned.1.call-start = ((), (), s32[]{:S(2)}) async-start(), calls=%async_computation.1 | async-start | bytes 589824 | tf_op jit(solution)/shard_map/reduce_scatter | solution.py:175
  188.5 7.7 copy-start.6
  207.8 12.6 copy-start.36
  219.5 810.8 %copy-start.28 = (f32[1,64,2,8,8]{1,0,4,3,2:T(1,128)S(1)}, f32[1,64,2,8,8]{1,0,4,3,2:T(1,128)}, u32[]{:S(2)}) copy-start(f32[1,64,2,8,8]{1,0,4,3,2:T(1,128)} %copy-done.27) | copy-start | bytes 98308
  219.5 810.8 %copy-start.33 = (f32[64]{0:T(128)S(1)}, f32[64]{0:T(128)}, u32[]{:S(2)}) copy-start(f32[64]{0:T(128)} %param.9) | copy-start | bytes 772
  220.4 1283.0 %all-reduce.13.cloned.1.call-start = ((), (), s32[]{:S(2)}) async-start(), calls=%async_computation.2 | async-start | bytes 2097152 | tf_op jit(solution)/shard_map/psum | solution.py:182
  1037.0 123.7 %copy-start.26 = (f32[64,32,1,2,1,2,1,2]{0,7,6,5,4,3,2,1:T(2,128)S(1)}, f32[64,32,1,2,1,2,1,2]{0,7,6,5,4,3,2,1:T(2,128)}, u32[]{:S(2)}) copy-start(f32[64,32,1,2,1,2,1,2]{0,7,6,5,4,3,2,1:T(2,128)} %get-tuple-element.55) | copy-start | bytes 196612
  1037.1 119.2 %collective-permute-start.2 = (f32[1,64,1,64]{1,3,2,0:T(8,128)S(1)}, f32[1,64,1,64]{1,3,2,0:T(8,128)S(1)}, u32[]{:S(2)}, u32[]{:S(2)}) collective-permute-start(f32[1,64,1,64]{1,3,2,0:T(8,128)S(1)} %get-tuple-element.74), channel_id=1, source_target_pairs={{0,1},{1,2},{2,3},{3,4},{4,5},{5,6},{6,7},{8,9},{9,10},{10,11},{11... | collective-permute-start | bytes 49160 | tf_op jit(solution)/shard_map/ppermute | solution.py:22
  1041.9 114.3 %collective-permute-start.3 = (f32[1,64,1,64]{1,3,2,0:T(8,128)S(1)}, f32[1,64,1,64]{1,3,2,0:T(8,128)S(1)}, u32[]{:S(2)}, u32[]{:S(2)}) collective-permute-start(f32[1,64,1,64]{1,3,2,0:T(8,128)S(1)} %get-tuple-element.75), channel_id=1, source_target_pairs={{1,0},{2,1},{3,2},{4,3},{5,4},{6,5},{7,6},{9,8},{10,9},{11,10},{12... | collective-permute-start | bytes 49160 | tf_op jit(solution)/shard_map/ppermute | solution.py:24
  1156.5 5.5 copy-start.24
  (12 other events, 22.6 us)
Sparse Core Ops, SparseCore 0:
  186.6 840.8 all-reduce.14
Sparse Core Ops, SparseCore 1:
  220.4 114.7 reduce-scatter.1
  1037.1 466.2 all-reduce.12
where the time goes:
time: 1520 us; the launch traced here: 1510 us
  waiting for transfers between devices  930 us (61%)
  blocking collectives  403 us (27%)
  local copies, waits for them, and re-layouts  106 us (7%)
  matrix products  29.1 us (2%)
  starting transfers between devices  24.6 us (2%)
  between operations  16.6 us (1%)
    psum x1, waiting for transfers between devices, on_device(): grad_w_second, grad_b_second = lax.psum((part_weight, part_bias), 'dp')  593 us
    psum x1, waiting for transfers between devices, on_device(): lax.psum((part_first, part_first_bias), ('dp', 'space'))  323 us
    psum x1, blocking collectives, on_device(): grad_w_second, grad_b_second = lax.psum((part_weight, part_bias), 'dp')  214 us
    psum x1, blocking collectives, on_device(): lax.psum((part_first, part_first_bias), ('dp', 'space'))  113 us
    all_gather x1, blocking collectives, on_device(): full_middle = lax.all_gather(layered, 'space', axis=2, tiled=True)  75.4 us
  transfers between devices with their start and end apart: 7, of which 3 were waited for; matrix products, arithmetic and copies ran while one was open for 4% of the time, Pallas kernels for 0%

commit v1 on v0

v1 whole, which is shorter than its diff:
```python
import functools

import jax
import jax.numpy as jnp
from jax import lax
from jax.experimental import pallas as pl
from jax.experimental.pallas import tpu as pltpu
from jax.sharding import PartitionSpec as P

MESH = pl.DeviceIdType.MESH
F32 = jnp.float32
BF16 = jnp.bfloat16
SLOPE = 0.3
CIN = 32
MID = 64
OWN = 8
SAMPLES = 64


def split(value):
    high = value.astype(BF16)
    low = (value - high.astype(F32)).astype(BF16)
    return high, low


def dot(a, b, contract):
    return lax.dot_general(a, b, ((contract[:1], contract[1:]), ((), ())), preferred_element_type=F32)


def smooth(pre):
    decay = jnp.exp(-jnp.abs(pre))
    soft = jnp.maximum(pre, 0.0) + jnp.log(1.0 + decay)
    return SLOPE * pre + (1.0 - SLOPE) * soft


def slope(pre):
    decay = jnp.exp(-jnp.abs(pre))
    return SLOPE + (1.0 - SLOPE) * (jnp.where(pre >= 0.0, 1.0, decay) / (1.0 + decay))


def source_of(column, tap, log_half):
    half = 1 << log_half
    width = 2 * half
    slab = lax.shift_right_logical(column, 2 * log_half)
    row = lax.shift_right_logical(column, log_half) & (half - 1)
    cell = column & (half - 1)
    high = 2 * row + lax.shift_right_logical(tap, 2) - 1
    low = 2 * cell + (tap & 3) - 1
    inside = (high >= 0) & (high < width) & (low >= 0) & (low < width)
    return jnp.where(inside, slab * (width * width) + high * width + low, -1)


def fill_pick(pick, log_half):
    @pl.loop(0, 8)
    def _(pair):
        lane = lax.broadcasted_iota(jnp.int32, (8, 256), 1)
        source = source_of(lane & 127, 2 * pair + lax.shift_right_logical(lane, 7), log_half)
        cell = lax.broadcasted_iota(jnp.int32, (512, 256), 0)
        pick[pair] = jnp.where(cell == source[0:1], 1.0, 0.0).astype(BF16)


def fill_spread(spread, log_half):
    @pl.loop(0, 8)
    def _(pair):
        row = lax.broadcasted_iota(jnp.int32, (256, 128), 0)
        source = source_of(row & 127, 2 * pair + lax.shift_right_logical(row, 7), log_half)
        cell = lax.broadcasted_iota(jnp.int32, (256, 128), 1)
        for part in range(4):
            spread[pair, :, part * 128 : (part + 1) * 128] = jnp.where(
                cell + part * 128 == source, 1.0, 0.0
            ).astype(BF16)


def columns(rows, pick, grid, channels):
    half = 4 * channels

    @pl.loop(0, 8)
    def _(pair):
        both = dot(rows[...], pick[pair], (1, 0))
        value = both[:half] + both[half:]
        for i in range(4):
            for second in range(2):
                grid[pl.ds(i * 16 + 2 * pair + second, channels, stride=64), :] = value[
                    i * channels : (i + 1) * channels, second * 128 : (second + 1) * 128
                ]


def forward(weights, grid, pair_grid, count, depth):
    chunk = 512

    def body(step, total):
        at = pl.multiple_of(step * chunk, chunk)
        high, low = split(grid[pl.ds(at, chunk), :])
        pair_grid[pl.ds(at, chunk), :128] = high
        pair_grid[pl.ds(at, chunk), 128:] = low
        return total + dot(weights[:, pl.ds(at, chunk)], pair_grid[pl.ds(at, chunk), :], (1, 0))

    total = lax.fori_loop(0, depth // chunk, body, jnp.zeros((2 * count, 256), F32))
    return (total[:count, :128] + total[:count, 128:]) + (total[count:, :128] + total[count:, 128:])


def kernel_grad(gradient, pair_grid, result, count, depth):
    chunk = 512
    high, low = split(gradient)
    both = jnp.concatenate(
        [jnp.concatenate([high, high], axis=1), jnp.concatenate([low, low], axis=1)], axis=0
    )

    @pl.loop(0, depth // chunk)
    def _(step):
        at = pl.multiple_of(step * chunk, chunk)
        value = dot(both, pair_grid[pl.ds(at, chunk), :], (1, 1))
        result[:, pl.ds(at, chunk)] = (value[:count] + value[count:]) * (1.0 / SAMPLES)


def column_grad(weights, gradient, grid, count, depth):
    chunk = 512
    high, low = split(gradient)
    both = jnp.concatenate(
        [jnp.concatenate([high, low], axis=1), jnp.concatenate([high, low], axis=1)], axis=0
    )

    @pl.loop(0, depth // chunk)
    def _(step):
        at = pl.multiple_of(step * chunk, chunk)
        value = dot(weights[:, pl.ds(at, chunk)], both, (0, 0))
        grid[pl.ds(at, chunk), :] = value[:, :128] + value[:, 128:]


def rows_grad(grid, spread, taps, total, channels):
    half = 4 * channels
    total[...] = jnp.zeros_like(total)

    @pl.loop(0, 8)
    def _(pair):
        for i in range(4):
            for second in range(2):
                high, low = split(grid[pl.ds(i * 16 + 2 * pair + second, channels, stride=64), :])
                lanes = slice(second * 128, (second + 1) * 128)
                taps[i * channels : (i + 1) * channels, lanes] = high
                taps[half + i * channels : half + (i + 1) * channels, lanes] = low
        both = dot(taps[...], spread[pair], (1, 0))
        total[...] += both[:half] + both[half:]


def copy_to(source, target, sends, receives, at, device):
    return pltpu.make_async_remote_copy(
        src_ref=source,
        dst_ref=target,
        send_sem=sends.at[at],
        recv_sem=receives.at[at],
        device_id=device,
        device_id_type=MESH,
    )


def layers_kernel(
    vol, cot, w1, b1, w2, b2,
    out, gw1, gw2, gbias, dvol,
    halo, hidden, pre1, dhidden, got, send_z, got_z,
    pick1, pick2, spread1, spread2,
    rows1, rows2, taps1, taps2, drows1, drows2,
    grid1, grid2, pairs1, pairs2, w1s, w2s,
    sends, receives,
):
    me = lax.axis_index("space")
    x, far = me // 2, me % 2
    barrier = pltpu.get_barrier_semaphore()
    for k in range(1, 8):
        pl.semaphore_signal(barrier, inc=1, device_id={"space": (me + k) % 8}, device_id_type=MESH)
    pl.semaphore_wait(barrier, 7)

    up = copy_to(vol.at[3], halo.at[0], sends, receives, 0, {"space": (me + 1) % 8})
    down = copy_to(vol.at[0], halo.at[1], sends, receives, 1, {"space": (me + 7) % 8})
    up.start()
    down.start()

    fill_pick(pick1, 3)
    fill_pick(pick2, 2)
    fill_spread(spread1, 3)
    fill_spread(spread2, 2)
    high, low = split(w1[...])
    w1s[:MID] = high
    w1s[MID:] = low
    high, low = split(w2[...])
    w2s[...] = jnp.concatenate([high, low], axis=0)

    def place(i, part, plane):
        high, low = split(plane)
        lanes = slice(part * 256, (part + 1) * 256)
        rows1[i * CIN : (i + 1) * CIN, lanes] = high
        rows1[4 * CIN + i * CIN : 4 * CIN + (i + 1) * CIN, lanes] = low

    for i in range(4):
        for part in range(2):
            if 0 <= 2 * part + i - 1 < 4:
                place(i, part, vol[2 * part + i - 1])
    up.wait()
    down.wait()
    place(0, 0, jnp.where(me > 0, halo[0], 0.0))
    place(3, 1, jnp.where(me < 7, halo[1], 0.0))
    columns(rows1, pick1, grid1, CIN)
    pre1[...] = forward(w1s, grid1, pairs1, MID, CIN * 64) + b1[...]
    hidden[me] = smooth(pre1[...])

    partner = 2 * x + 1 - far
    cross = copy_to(hidden.at[me], hidden.at[me], sends, receives, 2, {"space": partner})
    cross.start()
    own = []
    for k in range(1, 4):
        other = 2 * ((x + k) % 4) + far
        own.append(copy_to(hidden.at[me], hidden.at[me], sends, receives, 2 + k, {"space": other}))
        own[-1].start()
    cross.wait()
    for k in range(1, 4):
        other = 2 * ((x + k) % 4) + far
        own.append(
            copy_to(hidden.at[partner], hidden.at[partner], sends, receives, 5 + k, {"space": other})
        )
        own[-1].start()
    for copy in own:
        copy.wait()

    lane = lax.broadcasted_iota(jnp.int32, (MID, 128), 1)
    first = lane < 64
    zero = jnp.zeros((MID, 128), F32)

    def put(i, m, value):
        high, low = split(value)
        lanes = slice(m * 128, (m + 1) * 128)
        rows2[i * MID : (i + 1) * MID, lanes] = high
        rows2[4 * MID + i * MID : 4 * MID + (i + 1) * MID, lanes] = low

    for m in range(4):
        near, next_one = hidden[2 * m], hidden[2 * m + 1]
        before = hidden[2 * m - 1] if m > 0 else zero
        after = hidden[2 * m + 2] if m < 3 else zero
        put(0, m, jnp.where(first, pltpu.roll(before, 64, 1), near))
        put(1, m, jnp.where(first, near, pltpu.roll(next_one, 64, 1)))
        put(2, m, jnp.where(first, pltpu.roll(near, 64, 1), next_one))
        put(3, m, jnp.where(first, next_one, pltpu.roll(after, 64, 1)))
    columns(rows2, pick2, grid2, MID)
    pre2 = forward(w2s, grid2, pairs2, OWN, MID * 64) + b2[...]
    out[...] = smooth(pre2)
    grad2 = cot[...] * slope(pre2)
    column_grad(w2s, grad2, grid2, OWN, MID * 64)
    rows_grad(grid2, spread2, taps2, drows2, MID)

    def taken(i, m):
        if not 0 <= m < 4:
            return zero
        return drows2[i * MID : (i + 1) * MID, m * 128 : (m + 1) * 128]

    for m in range(4):
        dhidden[2 * m] = jnp.where(
            first,
            taken(1, m) + pltpu.roll(taken(3, m - 1), 64, 1),
            pltpu.roll(taken(2, m), 64, 1) + taken(0, m),
        )
        dhidden[2 * m + 1] = jnp.where(
            first,
            pltpu.roll(taken(1, m), 64, 1) + taken(3, m),
            taken(2, m) + pltpu.roll(taken(0, m + 1), 64, 1),
        )
    shares = []
    for k in range(1, 4):
        other = (x + k) % 4
        shares.append(
            copy_to(
                dhidden.at[pl.ds(2 * other, 2)], got.at[k - 1], sends, receives, 8 + k,
                {"space": 2 * other + far},
            )
        )
        shares[-1].start()
    kernel_grad(grad2, pairs2, gw2, OWN, MID * 64)
    for copy in shares:
        copy.wait()
    send_z[...] = (dhidden[partner] + got[0, 1 - far]) + (got[1, 1 - far] + got[2, 1 - far])
    cross = copy_to(send_z, got_z, sends, receives, 12, {"space": partner})
    cross.start()
    mine = (dhidden[me] + got[0, far]) + (got[1, far] + got[2, far])
    cross.wait()
    grad1 = (mine + got_z[...]) * slope(pre1[...])

    ones = jnp.ones((8, 128), BF16)

    def sums(value):
        high, low = split(value)
        rest = (value - high.astype(F32) - low.astype(F32)).astype(BF16)
        return (dot(ones, high, (1, 1)) + dot(ones, low, (1, 1)) + dot(ones, rest, (1, 1))) * (1.0 / SAMPLES)

    gbias[...] = jnp.zeros((8, 128), F32)
    gbias[:, :MID] = sums(grad1)
    gbias[:, MID : MID + OWN] = sums(grad2)
    kernel_grad(grad1, pairs1, gw1, MID, CIN * 64)
    column_grad(w1s, grad1, grid1, MID, CIN * 64)
    rows_grad(grid1, spread1, taps1, drows1, CIN)

    def back(i, part):
        return drows1[i * CIN : (i + 1) * CIN, part * 256 : (part + 1) * 256]

    dvol[0] = back(0, 0)
    dvol[1] = back(1, 0)
    dvol[2] = back(2, 0) + back(0, 1)
    dvol[3] = back(3, 0) + back(1, 1)
    dvol[4] = back(2, 1)
    dvol[5] = back(3, 1)


def layers(vol, cot, w1, b1, w2, b2):
    shape = jax.ShapeDtypeStruct
    return pl.pallas_call(
        layers_kernel,
        out_shape=(
            shape((OWN, 128), F32),
            shape((MID, CIN * 64), F32),
            shape((OWN, MID * 64), F32),
            shape((8, 128), F32),
            shape((6, CIN, 256), F32),
        ),
        in_specs=[pl.BlockSpec(memory_space=pltpu.VMEM)] * 6,
        out_specs=[pl.BlockSpec(memory_space=pltpu.VMEM)] * 5,
        scratch_shapes=[
            pltpu.VMEM((2, CIN, 256), F32),
            pltpu.VMEM((8, MID, 128), F32),
            pltpu.VMEM((MID, 128), F32),
            pltpu.VMEM((8, MID, 128), F32),
            pltpu.VMEM((3, 2, MID, 128), F32),
            pltpu.VMEM((MID, 128), F32),
            pltpu.VMEM((MID, 128), F32),
            pltpu.VMEM((8, 512, 256), BF16),
            pltpu.VMEM((8, 512, 256), BF16),
            pltpu.VMEM((8, 256, 512), BF16),
            pltpu.VMEM((8, 256, 512), BF16),
            pltpu.VMEM((8 * CIN, 512), BF16),
            pltpu.VMEM((8 * MID, 512), BF16),
            pltpu.VMEM((8 * CIN, 256), BF16),
            pltpu.VMEM((8 * MID, 256), BF16),
            pltpu.VMEM((4 * CIN, 512), F32),
            pltpu.VMEM((4 * MID, 512), F32),
            pltpu.VMEM((CIN * 64, 128), F32),
            pltpu.VMEM((MID * 64, 128), F32),
            pltpu.VMEM((CIN * 64, 256), BF16),
            pltpu.VMEM((MID * 64, 256), BF16),
            pltpu.VMEM((2 * MID, CIN * 64), BF16),
            pltpu.VMEM((2 * OWN, MID * 64), BF16),
            pltpu.SemaphoreType.DMA((13,)),
            pltpu.SemaphoreType.DMA((13,)),
        ],
        compiler_params=pltpu.CompilerParams(
            collective_id=0, has_side_effects=True, vmem_limit_bytes=48 << 20
        ),
        name="layers",
    )(vol, cot, w1, b1, w2, b2)


def flip(index, k):
    if k == 1:
        return index + 1 - 2 * (index % 2)
    if k == 2:
        return (index + 2) % 4
    return 3 - index


def reduce_kernel(
    gw1, gw2, gbias, dvol,
    tw1, tw2, tbias, tvol,
    halo, c1, c2, c3, s1, s2, s3, x1, x3, m1, m3, y1, y2, y3, n1, n2, n3,
    r1, r2, r3, o1, o2, o3, a1, a2, a3,
    sends, receives,
):
    dp, me = lax.axis_index("dp"), lax.axis_index("space")
    core, low, y = dp % 2, (dp // 2) % 8, dp // 16
    x, far = me // 2, me % 2
    run, step = 2 * far + low // 4, low % 4
    core_peer = {"dp": dp + 1 - 2 * core, "space": me}
    x_peers = [{"dp": dp, "space": 2 * flip(x, k) + far} for k in (1, 2, 3)]
    y_peers = [{"dp": flip(y, k) * 16 + dp % 16, "space": me} for k in (1, 2, 3)]
    b_peers = [
        {"dp": y * 16 + (4 * (low // 4) + flip(step, k)) * 2 + core, "space": me} for k in (1, 2, 3)
    ]
    a_peers = [
        {
            "dp": y * 16 + (4 * (flip(run, k) % 2) + step) * 2 + core,
            "space": 2 * x + flip(run, k) // 2,
        }
        for k in (1, 2, 3)
    ]
    above = {"dp": dp, "space": (me + 1) % 8}
    below = {"dp": dp, "space": (me + 7) % 8}
    barrier = pltpu.get_barrier_semaphore()
    peers = [core_peer, *x_peers, *y_peers, *b_peers, *a_peers, above, below]
    for peer in peers:
        pl.semaphore_signal(barrier, inc=1, device_id=peer, device_id_type=MESH)
    pl.semaphore_wait(barrier, len(peers))

    used = [0]

    def send(source, target, peer):
        copy = copy_to(source, target, sends, receives, used[0], peer)
        used[0] += 1
        copy.start()
        return copy

    def wait(copies):
        for copy in copies:
            copy.wait()

    lane = lax.broadcasted_iota(jnp.int32, (8, 128), 1)
    shared = lane < MID

    def rows(count, index):
        return pl.ds(pl.multiple_of(count * index, 8), count)

    def lanes(start, count):
        return pl.ds(pl.multiple_of(start, 128), count)

    edges = [send(dvol.at[0], halo.at[1], below), send(dvol.at[5], halo.at[0], above)]
    wait(
        [
            send(gw1.at[rows(32, 1 - core), :], c1, core_peer),
            send(gw2.at[:, lanes((1 - core) * 2048, 2048)], c2, core_peer),
            send(gbias, c3, core_peer),
        ]
    )
    s1[...] = gw1[rows(32, core), :] + c1[...]
    s2[...] = gw2[:, lanes(core * 2048, 2048)] + c2[...]
    s3[...] = gbias[...] + c3[...]
    copies = []
    for k in (1, 2, 3):
        copies.append(send(s1.at[rows(8, flip(x, k)), :], x1.at[k - 1], x_peers[k - 1]))
        copies.append(send(s3, x3.at[k - 1], x_peers[k - 1]))
    wait(copies)
    m1[...] = (s1[rows(8, x), :] + x1[0]) + (x1[1] + x1[2])
    m3[...] = jnp.where(shared, (s3[...] + x3[0]) + (x3[1] + x3[2]), s3[...])
    copies = []
    for k in (1, 2, 3):
        there = lanes(flip(y, k) * 512, 512)
        copies.append(send(m1.at[:, there], y1.at[k - 1], y_peers[k - 1]))
        copies.append(send(s2.at[:, there], y2.at[k - 1], y_peers[k - 1]))
        copies.append(send(m3, y3.at[k - 1], y_peers[k - 1]))
    wait(copies)
    here = lanes(y * 512, 512)
    n1[...] = (m1[:, here] + y1[0]) + (y1[1] + y1[2])
    n2[...] = (s2[:, here] + y2[0]) + (y2[1] + y2[2])
    n3[...] = (m3[...] + y3[0]) + (y3[1] + y3[2])
    copies = []
    for k in (1, 2, 3):
        there = lanes(flip(step, k) * 128, 128)
        copies.append(send(n1.at[:, there], r1.at[k - 1], b_peers[k - 1]))
        copies.append(send(n2.at[:, there], r2.at[k - 1], b_peers[k - 1]))
        copies.append(send(n3, r3.at[k - 1], b_peers[k - 1]))
    wait(copies)
    here = lanes(step * 128, 128)
    o1[...] = (n1[:, here] + r1[0]) + (r1[1] + r1[2])
    o2[...] = (n2[:, here] + r2[0]) + (r2[1] + r2[2])
    o3[...] = (n3[...] + r3[0]) + (r3[1] + r3[2])
    copies = [send(o2, a2, a_peers[0])]
    for k in (1, 2, 3):
        copies.append(send(o1, a1.at[k - 1], a_peers[k - 1]))
        copies.append(send(o3, a3.at[k - 1], a_peers[k - 1]))
    wait(copies)
    near = o3[...] + a3[0]
    tbias[...] = jnp.where(shared, near + (a3[1] + a3[2]), near)
    own_rows = rows(8, core * 4 + x)
    at1 = y * 512 + step * 128
    at2 = core * 2048 + at1
    tw1[own_rows, lanes(at1, 128)] = (o1[...] + a1[0]) + (a1[1] + a1[2])
    tw2[:, lanes(at2, 128)] = o2[...] + a2[...]
    copies = []
    for peer in b_peers:
        here1 = tw1.at[own_rows, lanes(at1, 128)]
        here2 = tw2.at[:, lanes(at2, 128)]
        copies += [send(here1, here1, peer), send(here2, here2, peer)]
    wait(copies)
    copies = []
    for peer in y_peers:
        here1 = tw1.at[own_rows, lanes(y * 512, 512)]
        here2 = tw2.at[:, lanes(core * 2048 + y * 512, 512)]
        copies += [send(here1, here1, peer), send(here2, here2, peer)]
    wait(copies)
    here2 = tw2.at[:, lanes(core * 2048, 2048)]
    last = [send(here2, here2, core_peer)]
    copies = []
    for peer in x_peers:
        here1 = tw1.at[own_rows, :]
        copies.append(send(here1, here1, peer))
    wait(copies)
    here1 = tw1.at[rows(32, core), :]
    last.append(send(here1, here1, core_peer))
    wait(edges)
    tvol[0] = dvol[1] + jnp.where(me > 0, halo[0], 0.0)
    tvol[1] = dvol[2]
    tvol[2] = dvol[3]
    tvol[3] = dvol[4] + jnp.where(me < 7, halo[1], 0.0)
    wait(last)


def reduced(gw1, gw2, gbias, dvol):
    shape = jax.ShapeDtypeStruct

    def vmem(*size):
        return pltpu.VMEM(size, F32)

    return pl.pallas_call(
        reduce_kernel,
        out_shape=(
            shape((MID, CIN * 64), F32),
            shape((OWN, MID * 64), F32),
            shape((8, 128), F32),
            shape((4, CIN, 256), F32),
        ),
        in_specs=[pl.BlockSpec(memory_space=pltpu.VMEM)] * 4,
        out_specs=[pl.BlockSpec(memory_space=pltpu.VMEM)] * 4,
        scratch_shapes=[
            vmem(2, CIN, 256),
            vmem(32, 2048), vmem(8, 2048), vmem(8, 128),
            vmem(32, 2048), vmem(8, 2048), vmem(8, 128),
            vmem(3, 8, 2048), vmem(3, 8, 128),
            vmem(8, 2048), vmem(8, 128),
            vmem(3, 8, 512), vmem(3, 8, 512), vmem(3, 8, 128),
            vmem(8, 512), vmem(8, 512), vmem(8, 128),
            vmem(3, 8, 128), vmem(3, 8, 128), vmem(3, 8, 128),
            vmem(8, 128), vmem(8, 128), vmem(8, 128),
            vmem(3, 8, 128), vmem(8, 128), vmem(3, 8, 128),
            pltpu.SemaphoreType.DMA((64,)),
            pltpu.SemaphoreType.DMA((64,)),
        ],
        compiler_params=pltpu.CompilerParams(
            collective_id=1, has_side_effects=True, vmem_limit_bytes=32 << 20
        ),
        name="reduced",
    )(gw1, gw2, gbias, dvol)


def on_device(volume, cotangent, w_first, b_first, w_second, b_second):
    vol = volume[0].transpose(1, 0, 2)
    out, gw1, gw2, gbias, dvol = layers(
        vol, cotangent[0], w_first, b_first[:, None], w_second, b_second[:, None]
    )
    gw1, gw2, gbias, dvol = reduced(gw1, gw2, gbias, dvol)
    return (
        out[None],
        dvol.transpose(1, 0, 2)[None],
        gw1,
        gbias[0, :MID],
        gw2,
        gbias[0, MID : MID + OWN],
    )


def solution(mesh):
    in_specs = (
        P("dp", None, "space", None),
        P("dp", "space", None),
        P(),
        P(),
        P("space", None),
        P("space"),
    )
    out_specs = (
        P("dp", "space", None),
        P("dp", None, "space", None),
        P(),
        P(),
        P("space", None),
        P("space"),
    )
    return jax.shard_map(
        on_device, mesh=mesh, in_specs=in_specs, out_specs=out_specs, check_vma=False
    )
```

time: 1520 us -> 121 us (0.08)
  waiting for transfers between devices: 930 us -> 0 us
  blocking collectives: 403 us -> 0 us
  Pallas kernels: 0 us -> 112 us
  local copies, waits for them, and re-layouts: 106 us -> 7.28 us
  matrix products: 29.1 us -> 0 us
  starting transfers between devices: 24.6 us -> 0 us
  between operations: 16.6 us -> 0.69 us
    psum x2 -> x0, waiting for transfers between devices: 915 us -> none  [the longest x1 593 us: on_device(): grad_w_second, grad_b_second = lax.psum((part_weight, part_bias), 'dp')]
    psum x2 -> x0, blocking collectives: 327 us -> none  [the longest x1 214 us: on_device(): grad_w_second, grad_b_second = lax.psum((part_weight, part_bias), 'dp')]
    pallas_call x0 -> x2, Pallas kernels: none -> 112 us  [the longest x1 60.2 us: layers(): pl.pallas_call(layers_kernel, out_shape=(shape((OWN, 128), F32), shape((M...]
    all_gather x1 -> x0, blocking collectives: 75.4 us -> none  [on_device(): full_middle = lax.all_gather(layered, 'space', axis=2, tiled=True)]
    transpose x4 -> x0, local copies, waits for them, and re-layouts: 42 us -> none  [the longest x2 22.5 us: to_blocks(): split_grid = split_grid.transpose(0, 1, 3, 5, 7, 2, 4, 6)]
    reshape x10 -> x0, local copies, waits for them, and re-layouts: 31.5 us -> none  [the longest x2 14.7 us: to_blocks(): split_grid.reshape(sample_count, channels * 8, grid_depth // 2 * (grid_he...]
    dot_general x48 -> x0, matrix products: 29.1 us -> none  [the longest x16 10.6 us: input_grad(): jnp.einsum('ok,sot->skt', tap_weight(weight, channels, a, b, c), window,...]
    ppermute x4 -> x0, starting transfers between devices: 24.3 us -> none  [the longest x2 21.7 us: padded_2(): lax.ppermute(tail, axis, [(i, (i + 1) % count) for i in range(ends)])]
  transfers between devices with their start and end apart: 7 -> 0, of which waited for: 3 -> 0; matrix products, arithmetic and copies ran while one was open for 4% -> 0% of each run, Pallas kernels for 0% -> 0%
where the time goes in v1:
time: 121 us; the launch traced here: 120 us
  Pallas kernels  112 us (93%)
  local copies, waits for them, and re-layouts  7.28 us (6%)
    pallas_call x1, Pallas kernels, layers(): pl.pallas_call(layers_kernel, out_shape=(shape((OWN, 128), F32), shape((M...  60.2 us
    pallas_call x1, Pallas kernels, reduced(): pl.pallas_call(reduce_kernel, out_shape=(shape((MID, CIN * 64), F32), sha...  52.2 us
    unnamed x15, local copies, waits for them, and re-layouts  6.02 us

profile of v1, /device:TPU:1, one launch (start us, length us, event | category | flops | bytes accessed | tf_op | source)
XLA Modules:
  0.0 120.3 jit_solution(13436589471815521737)
XLA Ops:
  0.6 0.0 copy-start.4
  0.6 0.6 copy-done.4
  1.3 0.0 copy-start.3
  1.3 0.1 copy.14.b2
  1.4 0.6 copy-done.3
  1.9 0.1 copy.13.b1
  2.0 0.0 copy-start.1
  2.0 0.0 copy-start.2
  2.0 1.0 copy.17
  3.0 0.0 copy-done.1
  3.0 0.0 copy-done.2
  3.0 0.0 copy-start
  3.1 1.0 copy-done
  4.1 60.2 %layers.1 = (f32[8,128]{1,0:T(8,128)S(1)}, f32[64,2048]{1,0:T(8,128)S(1)}, f32[8,4096]{1,0:T(8,128)S(1)}, f32[8,128]{1,0:T(8,128)S(1)}, f32[6,32,256]{2,1,0:T(8,128)S(1)}) custom-call(f32[4,32,256]{2,1,0:T(8,128)S(1)} %bitcast.16, f32[8,128]{1,0:T(8,128)S(1)} %bitcast.18, f32[64,2048]{1,0:T(8,128)S(1)} %copy-done, f32[64,1]{1,0:T(8,128)S(1)} %copy.13.b1, ...), custom_call_target="tpu_custom_call" | custom-call | tf_op jit(solution)/shard_map/layers/pallas_call | solution.py:312
  64.3 52.2 %reduced.1 = (f32[64,2048]{1,0:T(8,128)S(1)}, f32[8,4096]{1,0:T(8,128)S(1)}, f32[8,128]{1,0:T(8,128)S(1)}, f32[4,32,256]{2,1,0:T(8,128)S(1)}) custom-call(f32[64,2048]{1,0:T(8,128)S(1)} %get-tuple-element.16.gw1, f32[8,4096]{1,0:T(8,128)S(1)} %get-tuple-element.17.gw2, f32[8,128]{1,0:T(8,128)S(1)} %get-tuple-element.18.gbias, ...), custom_call_target="tpu_custom_call" | custom-call | tf_op jit(solution)/shard_map/reduced/pallas_call | solution.py:505
  116.5 0.7 copy.15
  117.2 0.6 slice_bitcast_fusion
  117.8 0.5 slice_bitcast_fusion.1
  118.3 0.6 copy.21
  118.9 0.8 copy.22
  119.7 0.7 copy.23
Async XLA Ops:
  0.6 0.7 copy-start.4
  1.3 0.7 copy-start.3
  2.0 1.0 copy-start.1
  2.0 1.0 copy-start.2
  3.0 1.0 copy-start

commit v2 on v1

v2 whole, which is shorter than its diff:
```python
import functools

import jax
import jax.numpy as jnp
from jax import lax
from jax.experimental import pallas as pl
from jax.experimental.pallas import tpu as pltpu
from jax.sharding import PartitionSpec as P

MESH = pl.DeviceIdType.MESH
F32 = jnp.float32
BF16 = jnp.bfloat16
SLOPE = 0.3
CIN = 32
MID = 64
OWN = 8
SAMPLES = 64
UNROLL = 4


def split(value):
    high = value.astype(BF16)
    low = (value - high.astype(F32)).astype(BF16)
    return high, low


def dot(a, b, contract):
    return lax.dot_general(a, b, ((contract[:1], contract[1:]), ((), ())), preferred_element_type=F32)


def smooth(pre):
    decay = jnp.exp(-jnp.abs(pre))
    soft = jnp.maximum(pre, 0.0) + jnp.log(1.0 + decay)
    return SLOPE * pre + (1.0 - SLOPE) * soft


def slope(pre):
    decay = jnp.exp(-jnp.abs(pre))
    return SLOPE + (1.0 - SLOPE) * (jnp.where(pre >= 0.0, 1.0, decay) / (1.0 + decay))


def source_of(column, tap, log_half):
    half = 1 << log_half
    width = 2 * half
    slab = lax.shift_right_logical(column, 2 * log_half)
    row = lax.shift_right_logical(column, log_half) & (half - 1)
    cell = column & (half - 1)
    high = 2 * row + lax.shift_right_logical(tap, 2) - 1
    low = 2 * cell + (tap & 3) - 1
    inside = (high >= 0) & (high < width) & (low >= 0) & (low < width)
    return jnp.where(inside, slab * (width * width) + high * width + low, -1)


def fill_pick(pick, log_half):
    @pl.loop(0, 8)
    def _(pair):
        lane = lax.broadcasted_iota(jnp.int32, (8, 256), 1)
        source = source_of(lane & 127, 2 * pair + lax.shift_right_logical(lane, 7), log_half)
        cell = lax.broadcasted_iota(jnp.int32, (512, 256), 0)
        pick[pair] = jnp.where(cell == source[0:1], 1.0, 0.0).astype(BF16)


def fill_spread(spread, log_half):
    @pl.loop(0, 8)
    def _(pair):
        row = lax.broadcasted_iota(jnp.int32, (256, 128), 0)
        source = source_of(row & 127, 2 * pair + lax.shift_right_logical(row, 7), log_half)
        cell = lax.broadcasted_iota(jnp.int32, (256, 128), 1)
        for part in range(4):
            spread[pair, :, part * 128 : (part + 1) * 128] = jnp.where(
                cell + part * 128 == source, 1.0, 0.0
            ).astype(BF16)


def columns(rows, pick, grid, channels):
    half = 4 * channels

    @pl.loop(0, 8, unroll=UNROLL)
    def _(pair):
        both = dot(rows[...], pick[pair], (1, 0))
        value = both[:half] + both[half:]
        for i in range(4):
            for second in range(2):
                grid[pl.ds(i * 16 + 2 * pair + second, channels, stride=64), :] = value[
                    i * channels : (i + 1) * channels, second * 128 : (second + 1) * 128
                ]


def forward(weights, grid, pair_grid, count, depth):
    chunk = 512

    def body(step, total):
        at = pl.multiple_of(step * chunk, chunk)
        high, low = split(grid[pl.ds(at, chunk), :])
        pair_grid[pl.ds(at, chunk), :128] = high
        pair_grid[pl.ds(at, chunk), 128:] = low
        return total + dot(weights[:, pl.ds(at, chunk)], pair_grid[pl.ds(at, chunk), :], (1, 0))

    total = lax.fori_loop(0, depth // chunk, body, jnp.zeros((2 * count, 256), F32), unroll=UNROLL)
    return (total[:count, :128] + total[:count, 128:]) + (total[count:, :128] + total[count:, 128:])


def kernel_grad(gradient, pair_grid, result, count, depth):
    chunk = 512
    high, low = split(gradient)
    both = jnp.concatenate(
        [jnp.concatenate([high, high], axis=1), jnp.concatenate([low, low], axis=1)], axis=0
    )

    @pl.loop(0, depth // chunk, unroll=UNROLL)
    def _(step):
        at = pl.multiple_of(step * chunk, chunk)
        value = dot(both, pair_grid[pl.ds(at, chunk), :], (1, 1))
        result[:, pl.ds(at, chunk)] = (value[:count] + value[count:]) * (1.0 / SAMPLES)


def column_grad(weights, gradient, grid, count, depth):
    chunk = 512
    high, low = split(gradient)
    both = jnp.concatenate(
        [jnp.concatenate([high, low], axis=1), jnp.concatenate([high, low], axis=1)], axis=0
    )

    @pl.loop(0, depth // chunk, unroll=UNROLL)
    def _(step):
        at = pl.multiple_of(step * chunk, chunk)
        value = dot(weights[:, pl.ds(at, chunk)], both, (0, 0))
        grid[pl.ds(at, chunk), :] = value[:, :128] + value[:, 128:]


def rows_grad(grid, spread, taps, total, channels):
    half = 4 * channels
    total[...] = jnp.zeros_like(total)

    @pl.loop(0, 8, unroll=UNROLL)
    def _(pair):
        for i in range(4):
            for second in range(2):
                high, low = split(grid[pl.ds(i * 16 + 2 * pair + second, channels, stride=64), :])
                lanes = slice(second * 128, (second + 1) * 128)
                taps[i * channels : (i + 1) * channels, lanes] = high
                taps[half + i * channels : half + (i + 1) * channels, lanes] = low
        both = dot(taps[...], spread[pair], (1, 0))
        total[...] += both[:half] + both[half:]


def fill_fold(fold):
    @pl.loop(0, 8)
    def _(pair):
        row = lax.broadcasted_iota(jnp.int32, (128, 128), 0)
        cell = source_of(row & 15, 2 * pair + lax.shift_right_logical(row, 6), 2)
        plane = lax.shift_right_logical(row, 5) & 1
        lane = lax.broadcasted_iota(jnp.int32, (128, 128), 1)
        fold[pair] = jnp.where((cell >= 0) & (lane == plane * 64 + cell), 1.0, 0.0).astype(BF16)


def own_columns(weights, gradient, me, grid, depth):
    chunk = 512
    lane = lax.broadcasted_iota(jnp.int32, (MID, 128), 1)
    near = pltpu.roll(gradient, (144 - 16 * me) % 128, 1)
    again = pltpu.roll(gradient, (176 - 16 * me) % 128, 1)
    chosen = jnp.where(lane < 48, near, again)
    outside = ((lane < 16) & (me == 0)) | ((lane >= 32) & (lane < 48) & (me == 7))
    high, low = split(jnp.where(outside, 0.0, chosen))
    packed = jnp.where(lane < 64, high.astype(F32), pltpu.roll(low.astype(F32), 64, 1)).astype(BF16)
    both = jnp.concatenate([packed, packed], axis=0)

    @pl.loop(0, depth // chunk, unroll=UNROLL)
    def _(step):
        at = pl.multiple_of(step * chunk, chunk)
        value = dot(weights[:, pl.ds(at, chunk)], both, (0, 0))
        grid[pl.ds(at, chunk), :] = value + pltpu.roll(value, 64, 1)


def own_planes(grid, fold, taps):
    lane = lax.broadcasted_iota(jnp.int32, (MID, 128), 1)
    slot = lax.shift_right_logical(lane, 4)

    def body(pair, total):
        value = jnp.zeros((MID, 128), F32)
        for second in range(2):
            for order, i in enumerate((3, 1, 0, 2)):
                part = grid[pl.ds(i * 16 + 2 * pair + second, MID, stride=64), :]
                value = jnp.where(slot == 4 * second + order, part, value)
        high, low = split(value)
        taps[pair, :MID] = high
        taps[pair, MID:] = low
        return total + dot(taps[pair], fold[pair], (1, 0))

    total = lax.fori_loop(0, 8, body, jnp.zeros((2 * MID, 128), F32), unroll=UNROLL)
    return total[:MID] + total[MID:]


def copy_to(source, target, sends, receives, at, device):
    return pltpu.make_async_remote_copy(
        src_ref=source,
        dst_ref=target,
        send_sem=sends.at[at],
        recv_sem=receives.at[at],
        device_id=device,
        device_id_type=MESH,
    )


def flip(index, k):
    if k == 1:
        return index + 1 - 2 * (index % 2)
    if k == 2:
        return (index + 2) % 4
    return 3 - index


def step_kernel(
    vol_in, cot_in, w1_in, b1, w2_in, b2,
    out, tw1, tw2, tbias, tvol,
    raw, planes, halo, hidden, pre1, pre2, grad2, w1, w2, bias2,
    pick1, pick2, spread1, fold,
    rows1, rows2, taps1, taps2, drows1,
    grid1, grid2, pairs1, pairs2, w1s, w2s,
    gw1, gw2, gbias, edge_out, edge_in, inner,
    c1, c2, c3, s1, s2, s3, x1, x3, m1, m3, y1, y2, y3, n1, n2, n3,
    r1, r2, r3, o1, o2, o3, a1, a2, a3,
    loads, sends, receives,
):
    dp, me = lax.axis_index("dp"), lax.axis_index("space")
    core, low, y = dp % 2, (dp // 2) % 8, dp // 16
    x, far = me // 2, me % 2
    run, step = 2 * far + low // 4, low % 4
    partner = 2 * x + 1 - far
    core_peer = {"dp": dp + 1 - 2 * core, "space": me}
    z_peer = {"dp": dp, "space": partner}
    mirror = {"dp": y * 16 + (7 - low) * 2 + core, "space": partner}
    x_peers = [{"dp": dp, "space": 2 * flip(x, k) + far} for k in (1, 2, 3)]
    y_peers = [{"dp": flip(y, k) * 16 + dp % 16, "space": me} for k in (1, 2, 3)]
    b_peers = [
        {"dp": y * 16 + (4 * (low // 4) + flip(step, k)) * 2 + core, "space": me} for k in (1, 2, 3)
    ]
    a_peers = [
        {
            "dp": y * 16 + (4 * (flip(run, k) % 2) + step) * 2 + core,
            "space": 2 * x + flip(run, k) // 2,
        }
        for k in (1, 2, 3)
    ]
    space_peers = [{"dp": dp, "space": (me + k) % 8} for k in range(1, 8)]
    above, below = space_peers[0], space_peers[6]
    barrier = pltpu.get_barrier_semaphore()
    peers = [*space_peers, core_peer, mirror, *y_peers, *b_peers, *a_peers]
    for peer in peers:
        pl.semaphore_signal(barrier, inc=1, device_id=peer, device_id_type=MESH)

    used = [0]

    def send(source, target, peer):
        copy = copy_to(source, target, sends, receives, used[0], peer)
        used[0] += 1
        copy.start()
        return copy

    def wait(copies):
        for copy in copies:
            copy.wait()

    def rows(count, index):
        return pl.ds(pl.multiple_of(count * index, 8), count)

    def lanes(start, count):
        return pl.ds(pl.multiple_of(start, 128), count)

    fetches = [
        pltpu.make_async_copy(vol_in, raw, loads.at[0]),
        pltpu.make_async_copy(cot_in, hidden.at[me, MID:], loads.at[1]),
        pltpu.make_async_copy(w2_in.at[:, lanes(core * 2048, 2048)], w2.at[core, me], loads.at[2]),
        pltpu.make_async_copy(w1_in, w1, loads.at[3]),
    ]
    for fetch in fetches:
        fetch.start()
    bias2[me] = jnp.broadcast_to(b2[...], (OWN, 128))
    fetches[0].wait()
    for p in range(4):
        planes[p] = raw[:, p, :]
    fill_pick(pick1, 3)
    fetches[1].wait()
    fetches[2].wait()
    pl.semaphore_wait(barrier, len(peers))

    edges = [send(planes.at[3], halo.at[0], above), send(planes.at[0], halo.at[1], below)]
    mine = w2.at[core, me]
    cross_w = [send(mine, mine, mirror), send(bias2.at[me], bias2.at[me], mirror)]
    own_w = []
    for peer in x_peers:
        own_w += [send(mine, mine, peer), send(bias2.at[me], bias2.at[me], peer)]

    def place(i, part, plane):
        high, low_part = split(plane)
        at = slice(part * 256, (part + 1) * 256)
        rows1[i * CIN : (i + 1) * CIN, at] = high
        rows1[4 * CIN + i * CIN : 4 * CIN + (i + 1) * CIN, at] = low_part

    for i in range(4):
        for part in range(2):
            if 0 <= 2 * part + i - 1 < 4:
                place(i, part, planes[2 * part + i - 1])
    fetches[3].wait()
    high, low_part = split(w1[...])
    w1s[:MID] = high
    w1s[MID:] = low_part
    fill_pick(pick2, 2)
    wait(edges)
    place(0, 0, jnp.where(me > 0, halo[0], 0.0))
    place(3, 1, jnp.where(me < 7, halo[1], 0.0))
    columns(rows1, pick1, grid1, CIN)
    pre1[...] = forward(w1s, grid1, pairs1, MID, CIN * 64) + b1[...]
    hidden[me, :MID] = smooth(pre1[...])

    mine = hidden.at[me]
    cross = send(mine, mine, z_peer)
    own = [send(mine, mine, peer) for peer in x_peers]
    wait(cross_w)
    other, other_bias = w2.at[core, partner], bias2.at[partner]
    for peer in x_peers:
        own_w += [send(other, other, peer), send(other_bias, other_bias, peer)]
    fill_fold(fold)
    fill_spread(spread1, 3)
    cross.wait()
    other = hidden.at[partner]
    own += [send(other, other, peer) for peer in x_peers]
    wait(own_w)
    half = w2.at[core]
    share = send(half, half, core_peer)

    def take_weights(part):
        for s in range(8):
            high, low_part = split(w2[part, s])
            at = lanes(part * 2048, 2048)
            w2s[s * OWN : (s + 1) * OWN, at] = high
            w2s[MID + s * OWN : MID + (s + 1) * OWN, at] = low_part

    take_weights(core)
    wait(own)

    lane = lax.broadcasted_iota(jnp.int32, (MID, 128), 1)
    first = lane < 64
    zero = jnp.zeros((MID, 128), F32)

    def put(i, m, value):
        high, low_part = split(value)
        at = slice(m * 128, (m + 1) * 128)
        rows2[i * MID : (i + 1) * MID, at] = high
        rows2[4 * MID + i * MID : 4 * MID + (i + 1) * MID, at] = low_part

    for m in range(4):
        near, next_one = hidden[2 * m, :MID], hidden[2 * m + 1, :MID]
        before = hidden[2 * m - 1, :MID] if m > 0 else zero
        after = hidden[2 * m + 2, :MID] if m < 3 else zero
        put(0, m, jnp.where(first, pltpu.roll(before, 64, 1), near))
        put(1, m, jnp.where(first, near, pltpu.roll(next_one, 64, 1)))
        put(2, m, jnp.where(first, pltpu.roll(near, 64, 1), next_one))
        put(3, m, jnp.where(first, next_one, pltpu.roll(after, 64, 1)))
    columns(rows2, pick2, grid2, MID)
    share.wait()
    take_weights(1 - core)
    total = forward(w2s, grid2, pairs2, MID, MID * 64)
    for s in range(8):
        block = slice(s * OWN, (s + 1) * OWN)
        value = total[block] + bias2[s]
        pre2[s] = value
        grad2[s] = hidden[s, MID:] * slope(value)
    all_grad2 = jnp.concatenate([grad2[s] for s in range(8)], axis=0)
    own_columns(w2s, all_grad2, me, grid2, MID * 64)
    grad1 = own_planes(grid2, fold, taps2) * slope(pre1[...])
    kernel_grad(grad1, pairs1, gw1, MID, CIN * 64)
    copies = [send(gw1.at[rows(32, 1 - core), :], c1, core_peer)]

    ones = jnp.ones((8, 128), BF16)

    def sums(value):
        high, low_part = split(value)
        rest = (value - high.astype(F32) - low_part.astype(F32)).astype(BF16)
        return (dot(ones, high, (1, 1)) + dot(ones, low_part, (1, 1)) + dot(ones, rest, (1, 1))) * (
            1.0 / SAMPLES
        )

    own_grad2 = grad2[me]
    gbias[...] = jnp.zeros((8, 128), F32)
    gbias[:, :MID] = sums(grad1)
    gbias[:, MID : MID + OWN] = sums(own_grad2)
    copies.append(send(gbias, c3, core_peer))
    wait(copies)
    s1[...] = gw1[rows(32, core), :] + c1[...]
    s3[...] = gbias[...] + c3[...]
    copies = []
    for k in (1, 2, 3):
        copies.append(send(s1.at[rows(8, flip(x, k)), :], x1.at[k - 1], x_peers[k - 1]))
        copies.append(send(s3, x3.at[k - 1], x_peers[k - 1]))
    kernel_grad(own_grad2, pairs2, gw2, OWN, MID * 64)
    early = send(gw2.at[:, lanes((1 - core) * 2048, 2048)], c2, core_peer)
    out[...] = smooth(pre2[me])
    column_grad(w1s, grad1, grid1, MID, CIN * 64)
    early.wait()
    s2[...] = gw2[:, lanes(core * 2048, 2048)] + c2[...]
    wait(copies)
    shared = lax.broadcasted_iota(jnp.int32, (8, 128), 1) < MID
    m1[...] = (s1[rows(8, x), :] + x1[0]) + (x1[1] + x1[2])
    m3[...] = jnp.where(shared, (s3[...] + x3[0]) + (x3[1] + x3[2]), s3[...])
    copies = []
    for k in (1, 2, 3):
        there = lanes(flip(y, k) * 512, 512)
        copies.append(send(m1.at[:, there], y1.at[k - 1], y_peers[k - 1]))
        copies.append(send(s2.at[:, there], y2.at[k - 1], y_peers[k - 1]))
        copies.append(send(m3, y3.at[k - 1], y_peers[k - 1]))
    rows_grad(grid1, spread1, taps1, drows1, CIN)
    wait(copies)
    here = lanes(y * 512, 512)
    n1[...] = (m1[:, here] + y1[0]) + (y1[1] + y1[2])
    n2[...] = (s2[:, here] + y2[0]) + (y2[1] + y2[2])
    n3[...] = (m3[...] + y3[0]) + (y3[1] + y3[2])
    copies = []
    for k in (1, 2, 3):
        there = lanes(flip(step, k) * 128, 128)
        copies.append(send(n1.at[:, there], r1.at[k - 1], b_peers[k - 1]))
        copies.append(send(n2.at[:, there], r2.at[k - 1], b_peers[k - 1]))
        copies.append(send(n3, r3.at[k - 1], b_peers[k - 1]))

    def back(i, part):
        return drows1[i * CIN : (i + 1) * CIN, part * 256 : (part + 1) * 256]

    edge_out[0] = back(0, 0)
    edge_out[1] = back(3, 1)
    edges = [send(edge_out.at[0], edge_in.at[1], below), send(edge_out.at[1], edge_in.at[0], above)]
    wait(copies)
    here = lanes(step * 128, 128)
    o1[...] = (n1[:, here] + r1[0]) + (r1[1] + r1[2])
    o2[...] = (n2[:, here] + r2[0]) + (r2[1] + r2[2])
    o3[...] = (n3[...] + r3[0]) + (r3[1] + r3[2])
    copies = []
    for k in (1, 2, 3):
        copies.append(send(o1, a1.at[k - 1], a_peers[k - 1]))
        copies.append(send(o3, a3.at[k - 1], a_peers[k - 1]))
    copies.append(send(o2, a2, a_peers[0]))
    tvol[:, 1, :] = back(2, 0) + back(0, 1)
    tvol[:, 2, :] = back(3, 0) + back(1, 1)
    inner[0] = back(1, 0)
    inner[1] = back(2, 1)
    wait(copies)
    near = o3[...] + a3[0]
    tbias[...] = jnp.where(shared, near + (a3[1] + a3[2]), near)
    own_rows = rows(8, core * 4 + x)
    at1 = y * 512 + step * 128
    at2 = core * 2048 + at1
    tw1[own_rows, lanes(at1, 128)] = (o1[...] + a1[0]) + (a1[1] + a1[2])
    tw2[:, lanes(at2, 128)] = o2[...] + a2[...]
    copies = []
    for peer in b_peers:
        here1 = tw1.at[own_rows, lanes(at1, 128)]
        here2 = tw2.at[:, lanes(at2, 128)]
        copies += [send(here1, here1, peer), send(here2, here2, peer)]
    wait(edges)
    tvol[:, 0, :] = inner[0] + jnp.where(me > 0, edge_in[0], 0.0)
    tvol[:, 3, :] = inner[1] + jnp.where(me < 7, edge_in[1], 0.0)
    wait(copies)
    copies = []
    for peer in y_peers:
        here1 = tw1.at[own_rows, lanes(y * 512, 512)]
        here2 = tw2.at[:, lanes(core * 2048 + y * 512, 512)]
        copies += [send(here1, here1, peer), send(here2, here2, peer)]
    wait(copies)
    here2 = tw2.at[:, lanes(core * 2048, 2048)]
    last = [send(here2, here2, core_peer)]
    here1 = tw1.at[own_rows, :]
    copies = [send(here1, here1, peer) for peer in x_peers]
    last.append(send(here1, here1, core_peer))
    for k, copy in zip((1, 2, 3), copies):
        copy.wait()
        here1 = tw1.at[rows(8, core * 4 + flip(x, k)), :]
        last.append(send(here1, here1, core_peer))
    wait(last)


def stepped(vol, cot, w1, b1, w2, b2):
    shape = jax.ShapeDtypeStruct

    def vmem(*size):
        return pltpu.VMEM(size, F32)

    def half(*size):
        return pltpu.VMEM(size, BF16)

    return pl.pallas_call(
        step_kernel,
        out_shape=(
            shape((OWN, 128), F32),
            shape((MID, CIN * 64), F32),
            shape((OWN, MID * 64), F32),
            shape((8, 128), F32),
            shape((CIN, 4, 256), F32),
        ),
        in_specs=[
            pl.BlockSpec(memory_space=pltpu.HBM),
            pl.BlockSpec(memory_space=pltpu.HBM),
            pl.BlockSpec(memory_space=pltpu.HBM),
            pl.BlockSpec(memory_space=pltpu.VMEM),
            pl.BlockSpec(memory_space=pltpu.HBM),
            pl.BlockSpec(memory_space=pltpu.VMEM),
        ],
        out_specs=[pl.BlockSpec(memory_space=pltpu.VMEM)] * 5,
        scratch_shapes=[
            vmem(CIN, 4, 256), vmem(4, CIN, 256), vmem(2, CIN, 256),
            vmem(8, MID + OWN, 128), vmem(MID, 128), vmem(8, OWN, 128), vmem(8, OWN, 128),
            vmem(MID, CIN * 64), vmem(2, 8, OWN, 2048), vmem(8, OWN, 128),
            half(8, 512, 256), half(8, 512, 256), half(8, 256, 512), half(8, 128, 128),
            half(8 * CIN, 512), half(8 * MID, 512), half(8 * CIN, 256), half(8, 2 * MID, 128),
            vmem(4 * CIN, 512),
            vmem(CIN * 64, 128), vmem(MID * 64, 128), half(CIN * 64, 256), half(MID * 64, 256),
            half(2 * MID, CIN * 64), half(2 * MID, MID * 64),
            vmem(MID, CIN * 64), vmem(OWN, MID * 64), vmem(8, 128),
            vmem(2, CIN, 256), vmem(2, CIN, 256), vmem(2, CIN, 256),
            vmem(32, 2048), vmem(8, 2048), vmem(8, 128),
            vmem(32, 2048), vmem(8, 2048), vmem(8, 128),
            vmem(3, 8, 2048), vmem(3, 8, 128),
            vmem(8, 2048), vmem(8, 128),
            vmem(3, 8, 512), vmem(3, 8, 512), vmem(3, 8, 128),
            vmem(8, 512), vmem(8, 512), vmem(8, 128),
            vmem(3, 8, 128), vmem(3, 8, 128), vmem(3, 8, 128),
            vmem(8, 128), vmem(8, 128), vmem(8, 128),
            vmem(3, 8, 128), vmem(8, 128), vmem(3, 8, 128),
            pltpu.SemaphoreType.DMA((4,)),
            pltpu.SemaphoreType.DMA((96,)),
            pltpu.SemaphoreType.DMA((96,)),
        ],
        compiler_params=pltpu.CompilerParams(
            collective_id=0, has_side_effects=True, vmem_limit_bytes=60 << 20
        ),
        name="stepped",
    )(vol, cot, w1, b1, w2, b2)


def finish_kernel(out, gw1, gw2, gbias, gvol, to_out, to_w1, to_w2, to_b1, to_b2, to_vol, done):
    copies = [
        pltpu.make_async_copy(source, target, done.at[at])
        for at, (source, target) in enumerate(
            [(gw1, to_w1), (gw2, to_w2), (gvol, to_vol), (out, to_out)]
        )
    ]
    for copy in copies:
        copy.start()
    to_b1[...] = gbias[0, :MID]
    to_b2[...] = gbias[0, MID : MID + OWN]
    for copy in copies:
        copy.wait()


def finished(out, gw1, gw2, gbias, gvol):
    shape = jax.ShapeDtypeStruct
    anywhere = pl.BlockSpec(memory_space=pltpu.HBM)
    vmem = pl.BlockSpec(memory_space=pltpu.VMEM)
    return pl.pallas_call(
        finish_kernel,
        out_shape=(
            shape((OWN, 128), F32),
            shape((MID, CIN * 64), F32),
            shape((OWN, MID * 64), F32),
            shape((MID,), F32),
            shape((OWN,), F32),
            shape((CIN, 4, 256), F32),
        ),
        in_specs=[vmem] * 5,
        out_specs=[anywhere, anywhere, anywhere, vmem, vmem, anywhere],
        scratch_shapes=[pltpu.SemaphoreType.DMA((4,))],
        name="finished",
    )(out, gw1, gw2, gbias, gvol)


def on_device(volume, cotangent, w_first, b_first, w_second, b_second):
    results = stepped(
        volume[0], cotangent[0], w_first, b_first[:, None], w_second, b_second[:, None]
    )
    out, gw1, gw2, gb1, gb2, gvol = finished(*results)
    return (out[None], gvol[None], gw1, gb1, gw2, gb2)


def solution(mesh):
    in_specs = (
        P("dp", None, "space", None),
        P("dp", "space", None),
        P(),
        P(),
        P("space", None),
        P("space"),
    )
    out_specs = (
        P("dp", "space", None),
        P("dp", None, "space", None),
        P(),
        P(),
        P("space", None),
        P("space"),
    )
    return jax.shard_map(
        on_device, mesh=mesh, in_specs=in_specs, out_specs=out_specs, check_vma=False
    )
```

time: 121 us -> 96.7 us (0.80)
  Pallas kernels: 112 us -> 93.7 us
  local copies, waits for them, and re-layouts: 7.28 us -> 2.03 us
    pallas_call x2, Pallas kernels: 112 us -> 93.7 us  [the longest x1 91.2 us: stepped(): pl.pallas_call(step_kernel, out_shape=(shape((OWN, 128), F32), shape((MID...]
    unnamed x15 -> x4, local copies, waits for them, and re-layouts: 6.02 us -> 0.65 us
where the time goes in v2:
time: 96.7 us; the launch traced here: 96.4 us
  Pallas kernels  93.7 us (97%)
  local copies, waits for them, and re-layouts  2.03 us (2%)
    pallas_call x1, Pallas kernels, stepped(): pl.pallas_call(step_kernel, out_shape=(shape((OWN, 128), F32), shape((MID...  91.2 us
    pallas_call x1, Pallas kernels, finished(): pl.pallas_call(finish_kernel, out_shape=(shape((OWN, 128), F32), shape((M...  2.53 us

profile of v2, /device:TPU:1, one launch (start us, length us, event | category | flops | bytes accessed | tf_op | source)
XLA Modules:
  0.0 96.4 jit_solution(8964327359492345522)
XLA Ops:
  0.6 0.0 copy-start.1
  0.6 0.6 copy-done.1
  1.3 0.0 copy-start
  1.3 0.7 copy.13.b2
  2.0 0.0 copy-done
  2.0 0.7 copy.12.b1
  2.7 91.2 %stepped.1 = (f32[8,128]{1,0:T(8,128)}, f32[64,2048]{1,0:T(8,128)}, f32[8,4096]{1,0:T(8,128)}, f32[8,128]{1,0:T(8,128)}, f32[32,4,256]{2,1,0:T(4,128)}) custom-call(f32[32,4,256]{2,1,0:T(4,128)} %bitcast.6, f32[8,128]{1,0:T(8,128)} %bitcast.7, f32[64,2048]{1,0:T(8,128)} %w1_in.1, f32[64,1]{1,0:T(8,128)} %copy.12.b1, f32[8,4096]{1,0:T(8,128)} %w2_in.1, ...), custom_call_target="tpu_custom_call" | custom-call | tf_op jit(solution)/shard_map/stepped/pallas_call | solution.py:489
  93.9 2.5 %finished.1 = (f32[8,128]{1,0:T(8,128)}, f32[64,2048]{1,0:T(8,128)}, f32[8,4096]{1,0:T(8,128)}, f32[64]{0:T(128)}, f32[8]{0:T(128)}, /*index=5*/f32[32,4,256]{2,1,0:T(4,128)}) custom-call(f32[8,128]{1,0:T(8,128)} %get-tuple-element.17.out, f32[64,2048]{1,0:T(8,128)} %get-tuple-element.18.gw1, f32[8,4096]{1,0:T(8,128)} %get-tuple-element.19.gw2, ...), custom_call_target="tpu_custom_call" | custom-call | tf_op jit(solution)/shard_map/finished/pallas_call | solution.py:557
Async XLA Ops:
  0.6 0.7 copy-start.1
  1.3 0.7 copy-start

commit v3 on v2

--- a/solution.py
+++ b/solution.py
@@ -203,6 +203,8 @@
 
 
 def flip(index, k):
+    if k == 0:
+        return index
     if k == 1:
         return index + 1 - 2 * (index % 2)
     if k == 2:
@@ -211,14 +213,14 @@
 
 
 def step_kernel(
-    vol_in, cot_in, w1_in, b1, w2_in, b2,
+    vol_in, cot_in, w1_in, b1_in, w2_in, b2_in,
     out, tw1, tw2, tbias, tvol,
-    raw, planes, halo, hidden, pre1, pre2, grad2, w1, w2, bias2,
+    raw, planes, halo, hidden, pre1, pre2, grad2, w1, w2, bias1, bias2, row1, row2,
     pick1, pick2, spread1, fold,
     rows1, rows2, taps1, taps2, drows1,
     grid1, grid2, pairs1, pairs2, w1s, w2s,
-    gw1, gw2, gbias, edge_out, edge_in, inner,
-    c1, c2, c3, s1, s2, s3, x1, x3, m1, m3, y1, y2, y3, n1, n2, n3,
+    grad1, gw1, gw1_own, gw2, gbias, edge_out, edge_in, inner,
+    c1, c2, c3, s1, s2, s3, xy1, x3, m3, y2, y3, n1, n2, n3,
     r1, r2, r3, o1, o2, o3, a1, a2, a3,
     loads, sends, receives,
 ):
@@ -232,6 +234,12 @@
     mirror = {"dp": y * 16 + (7 - low) * 2 + core, "space": partner}
     x_peers = [{"dp": dp, "space": 2 * flip(x, k) + far} for k in (1, 2, 3)]
     y_peers = [{"dp": flip(y, k) * 16 + dp % 16, "space": me} for k in (1, 2, 3)]
+    xy_peers = {
+        (i, j): {"dp": flip(y, j) * 16 + dp % 16, "space": 2 * flip(x, i) + far}
+        for i in range(4)
+        for j in range(4)
+        if i or j
+    }
     b_peers = [
         {"dp": y * 16 + (4 * (low // 4) + flip(step, k)) * 2 + core, "space": me} for k in (1, 2, 3)
     ]
@@ -245,7 +253,8 @@
     space_peers = [{"dp": dp, "space": (me + k) % 8} for k in range(1, 8)]
     above, below = space_peers[0], space_peers[6]
     barrier = pltpu.get_barrier_semaphore()
-    peers = [*space_peers, core_peer, mirror, *y_peers, *b_peers, *a_peers]
+    peers = [*space_peers, core_peer, mirror, *b_peers, *a_peers]
+    peers += [peer for (_, j), peer in xy_peers.items() if j]
     for peer in peers:
         pl.semaphore_signal(barrier, inc=1, device_id=peer, device_id_type=MESH)
 
@@ -270,26 +279,42 @@
     fetches = [
         pltpu.make_async_copy(vol_in, raw, loads.at[0]),
         pltpu.make_async_copy(cot_in, hidden.at[me, MID:], loads.at[1]),
-        pltpu.make_async_copy(w2_in.at[:, lanes(core * 2048, 2048)], w2.at[core, me], loads.at[2]),
+        pltpu.make_async_copy(
+            w2_in.at[:, lanes(core * 2048 + y * 512, 512)], w2.at[core, y, me], loads.at[2]
+        ),
         pltpu.make_async_copy(w1_in, w1, loads.at[3]),
+        pltpu.make_async_copy(b1_in, row1, loads.at[4]),
+        pltpu.make_async_copy(b2_in, row2, loads.at[5]),
     ]
     for fetch in fetches:
         fetch.start()
-    bias2[me] = jnp.broadcast_to(b2[...], (OWN, 128))
+
+    def as_column(row, count):
+        down = lax.broadcasted_iota(jnp.int32, (count, count), 0)
+        along = lax.broadcasted_iota(jnp.int32, (count, count), 1)
+        diagonal = jnp.where(down == along, jnp.broadcast_to(row, (count, count)), 0.0)
+        return jnp.broadcast_to(jnp.sum(diagonal, axis=1, keepdims=True), (count, 128))
+
     fetches[0].wait()
-    for p in range(4):
-        planes[p] = raw[:, p, :]
-    fill_pick(pick1, 3)
-    fetches[1].wait()
+    planes[0] = raw[:, 0, :]
+    planes[3] = raw[:, 3, :]
+    pl.semaphore_wait(barrier, len(peers))
+
+    edges = [send(planes.at[3], halo.at[0], above), send(planes.at[0], halo.at[1], below)]
     fetches[2].wait()
-    pl.semaphore_wait(barrier, len(peers))
-
-    edges = [send(planes.at[3], halo.at[0], above), send(planes.at[0], halo.at[1], below)]
-    mine = w2.at[core, me]
-    cross_w = [send(mine, mine, mirror), send(bias2.at[me], bias2.at[me], mirror)]
+    fetches[5].wait()
+    bias2[me] = as_column(row2[...], OWN)
+    mine, mine_bias = w2.at[core, y, me], bias2.at[me]
+    cross_w = [send(mine, mine, mirror), send(mine_bias, mine_bias, mirror)]
     own_w = []
     for peer in x_peers:
-        own_w += [send(mine, mine, peer), send(bias2.at[me], bias2.at[me], peer)]
+        own_w += [send(mine, mine, peer), send(mine_bias, mine_bias, peer)]
+    fill_pick(pick1, 3)
+    planes[1] = raw[:, 1, :]
+    planes[2] = raw[:, 2, :]
+    fetches[4].wait()
+    bias1[...] = as_column(row1[...], MID)
+    fetches[1].wait()
 
     def place(i, part, plane):
         high, low_part = split(plane)
@@ -310,31 +335,35 @@
     place(0, 0, jnp.where(me > 0, halo[0], 0.0))
     place(3, 1, jnp.where(me < 7, halo[1], 0.0))
     columns(rows1, pick1, grid1, CIN)
-    pre1[...] = forward(w1s, grid1, pairs1, MID, CIN * 64) + b1[...]
+    wait(cross_w)
+    other, other_bias = w2.at[core, y, partner], bias2.at[partner]
+    for peer in x_peers:
+        own_w += [send(other, other, peer), send(other_bias, other_bias, peer)]
+    pre1[...] = forward(w1s, grid1, pairs1, MID, CIN * 64) + bias1[...]
     hidden[me, :MID] = smooth(pre1[...])
 
     mine = hidden.at[me]
     cross = send(mine, mine, z_peer)
     own = [send(mine, mine, peer) for peer in x_peers]
-    wait(cross_w)
-    other, other_bias = w2.at[core, partner], bias2.at[partner]
-    for peer in x_peers:
-        own_w += [send(other, other, peer), send(other_bias, other_bias, peer)]
+    wait(own_w)
+    mine = w2.at[core, y]
+    spread_w = [send(mine, mine, peer) for peer in y_peers]
     fill_fold(fold)
     fill_spread(spread1, 3)
     cross.wait()
     other = hidden.at[partner]
     own += [send(other, other, peer) for peer in x_peers]
-    wait(own_w)
+    wait(spread_w)
     half = w2.at[core]
     share = send(half, half, core_peer)
 
     def take_weights(part):
-        for s in range(8):
-            high, low_part = split(w2[part, s])
-            at = lanes(part * 2048, 2048)
-            w2s[s * OWN : (s + 1) * OWN, at] = high
-            w2s[MID + s * OWN : MID + (s + 1) * OWN, at] = low_part
+        for quarter in range(4):
+            for s in range(8):
+                high, low_part = split(w2[part, quarter, s])
+                at = lanes(part * 2048 + quarter * 512, 512)
+                w2s[s * OWN : (s + 1) * OWN, at] = high
+                w2s[MID + s * OWN : MID + (s + 1) * OWN, at] = low_part
 
     take_weights(core)
     wait(own)
@@ -368,9 +397,10 @@
         grad2[s] = hidden[s, MID:] * slope(value)
     all_grad2 = jnp.concatenate([grad2[s] for s in range(8)], axis=0)
     own_columns(w2s, all_grad2, me, grid2, MID * 64)
-    grad1 = own_planes(grid2, fold, taps2) * slope(pre1[...])
-    kernel_grad(grad1, pairs1, gw1, MID, CIN * 64)
-    copies = [send(gw1.at[rows(32, 1 - core), :], c1, core_peer)]
+    grad1[...] = own_planes(grid2, fold, taps2) * slope(pre1[...])
+    kernel_grad(grad1[rows(32, 1 - core), :], pairs1, gw1, 32, CIN * 64)
+    copies = [send(gw1, c1, core_peer)]
+    kernel_grad(grad1[rows(32, core), :], pairs1, gw1_own, 32, CIN * 64)
 
     ones = jnp.ones((8, 128), BF16)
 
@@ -383,68 +413,64 @@
 
     own_grad2 = grad2[me]
     gbias[...] = jnp.zeros((8, 128), F32)
-    gbias[:, :MID] = sums(grad1)
+    gbias[:, :MID] = sums(grad1[...])
     gbias[:, MID : MID + OWN] = sums(own_grad2)
     copies.append(send(gbias, c3, core_peer))
     wait(copies)
-    s1[...] = gw1[rows(32, core), :] + c1[...]
+    s1[...] = gw1_own[...] + c1[...]
     s3[...] = gbias[...] + c3[...]
     copies = []
-    for k in (1, 2, 3):
-        copies.append(send(s1.at[rows(8, flip(x, k)), :], x1.at[k - 1], x_peers[k - 1]))
-        copies.append(send(s3, x3.at[k - 1], x_peers[k - 1]))
+    for at, ((i, j), peer) in enumerate(xy_peers.items()):
+        piece = s1.at[rows(8, flip(x, i)), lanes(flip(y, j) * 512, 512)]
+        copies.append(send(piece, xy1.at[at], peer))
+    copies += [send(s3, x3.at[k], x_peers[k]) for k in range(3)]
     kernel_grad(own_grad2, pairs2, gw2, OWN, MID * 64)
     early = send(gw2.at[:, lanes((1 - core) * 2048, 2048)], c2, core_peer)
-    out[...] = smooth(pre2[me])
-    column_grad(w1s, grad1, grid1, MID, CIN * 64)
     early.wait()
     s2[...] = gw2[:, lanes(core * 2048, 2048)] + c2[...]
+    for k in (1, 2, 3):
+        piece = s2.at[:, lanes(flip(y, k) * 512, 512)]
+        copies.append(send(piece, y2.at[k - 1], y_peers[k - 1]))
+    column_grad(w1s, grad1[...], grid1, MID, CIN * 64)
+    out[...] = smooth(pre2[me])
     wait(copies)
     shared = lax.broadcasted_iota(jnp.int32, (8, 128), 1) < MID
-    m1[...] = (s1[rows(8, x), :] + x1[0]) + (x1[1] + x1[2])
+    here = lanes(y * 512, 512)
+    total = s1[rows(8, x), here] + xy1[0]
+    for at in range(1, 15):
+        total = total + xy1[at]
+    n1[...] = total
+    n2[...] = (s2[:, here] + y2[0]) + (y2[1] + y2[2])
     m3[...] = jnp.where(shared, (s3[...] + x3[0]) + (x3[1] + x3[2]), s3[...])
-    copies = []
-    for k in (1, 2, 3):
-        there = lanes(flip(y, k) * 512, 512)
-        copies.append(send(m1.at[:, there], y1.at[k - 1], y_peers[k - 1]))
-        copies.append(send(s2.at[:, there], y2.at[k - 1], y_peers[k - 1]))
-        copies.append(send(m3, y3.at[k - 1], y_peers[k - 1]))
-    rows_grad(grid1, spread1, taps1, drows1, CIN)
-    wait(copies)
-    here = lanes(y * 512, 512)
-    n1[...] = (m1[:, here] + y1[0]) + (y1[1] + y1[2])
-    n2[...] = (s2[:, here] + y2[0]) + (y2[1] + y2[2])
-    n3[...] = (m3[...] + y3[0]) + (y3[1] + y3[2])
     copies = []
     for k in (1, 2, 3):
         there = lanes(flip(step, k) * 128, 128)
         copies.append(send(n1.at[:, there], r1.at[k - 1], b_peers[k - 1]))
         copies.append(send(n2.at[:, there], r2.at[k - 1], b_peers[k - 1]))
-        copies.append(send(n3, r3.at[k - 1], b_peers[k - 1]))
-
+        copies.append(send(m3, y3.at[k - 1], y_peers[k - 1]))
     def back(i, part):
         return drows1[i * CIN : (i + 1) * CIN, part * 256 : (part + 1) * 256]
 
-    edge_out[0] = back(0, 0)
-    edge_out[1] = back(3, 1)
-    edges = [send(edge_out.at[0], edge_in.at[1], below), send(edge_out.at[1], edge_in.at[0], above)]
     wait(copies)
     here = lanes(step * 128, 128)
     o1[...] = (n1[:, here] + r1[0]) + (r1[1] + r1[2])
     o2[...] = (n2[:, here] + r2[0]) + (r2[1] + r2[2])
-    o3[...] = (n3[...] + r3[0]) + (r3[1] + r3[2])
+    n3[...] = (m3[...] + y3[0]) + (y3[1] + y3[2])
     copies = []
     for k in (1, 2, 3):
         copies.append(send(o1, a1.at[k - 1], a_peers[k - 1]))
-        copies.append(send(o3, a3.at[k - 1], a_peers[k - 1]))
+        copies.append(send(n3, r3.at[k - 1], b_peers[k - 1]))
     copies.append(send(o2, a2, a_peers[0]))
+    rows_grad(grid1, spread1, taps1, drows1, CIN)
+    edge_out[0] = back(0, 0)
+    edge_out[1] = back(3, 1)
+    edges = [send(edge_out.at[0], edge_in.at[1], below), send(edge_out.at[1], edge_in.at[0], above)]
     tvol[:, 1, :] = back(2, 0) + back(0, 1)
     tvol[:, 2, :] = back(3, 0) + back(1, 1)
     inner[0] = back(1, 0)
     inner[1] = back(2, 1)
     wait(copies)
-    near = o3[...] + a3[0]
-    tbias[...] = jnp.where(shared, near + (a3[1] + a3[2]), near)
+    o3[...] = (n3[...] + r3[0]) + (r3[1] + r3[2])
     own_rows = rows(8, core * 4 + x)
     at1 = y * 512 + step * 128
     at2 = core * 2048 + at1
@@ -455,25 +481,26 @@
         here1 = tw1.at[own_rows, lanes(at1, 128)]
         here2 = tw2.at[:, lanes(at2, 128)]
         copies += [send(here1, here1, peer), send(here2, here2, peer)]
+    copies += [send(o3, a3.at[k], a_peers[k]) for k in range(3)]
+    wait(copies)
+    piece1 = tw1.at[own_rows, lanes(y * 512, 512)]
+    piece2 = tw2.at[:, lanes(core * 2048 + y * 512, 512)]
+    back1 = {at: send(piece1, piece1, peer) for at, peer in xy_peers.items()}
+    back2 = [send(piece2, piece2, peer) for peer in y_peers]
+    near = o3[...] + a3[0]
+    tbias[...] = jnp.where(shared, near + (a3[1] + a3[2]), near)
+    wait(back2)
+    here2 = tw2.at[:, lanes(core * 2048, 2048)]
+    last = [send(here2, here2, core_peer)]
+    for i in range(4):
+        for j in range(4):
+            if i or j:
+                back1[i, j].wait()
+        here1 = tw1.at[rows(8, core * 4 + flip(x, i)), :]
+        last.append(send(here1, here1, core_peer))
     wait(edges)
     tvol[:, 0, :] = inner[0] + jnp.where(me > 0, edge_in[0], 0.0)
     tvol[:, 3, :] = inner[1] + jnp.where(me < 7, edge_in[1], 0.0)
-    wait(copies)
-    copies = []
-    for peer in y_peers:
-        here1 = tw1.at[own_rows, lanes(y * 512, 512)]
-        here2 = tw2.at[:, lanes(core * 2048 + y * 512, 512)]
-        copies += [send(here1, here1, peer), send(here2, here2, peer)]
-    wait(copies)
-    here2 = tw2.at[:, lanes(core * 2048, 2048)]
-    last = [send(here2, here2, core_peer)]
-    here1 = tw1.at[own_rows, :]
-    copies = [send(here1, here1, peer) for peer in x_peers]
-    last.append(send(here1, here1, core_peer))
-    for k, copy in zip((1, 2, 3), copies):
-        copy.wait()
-        here1 = tw1.at[rows(8, core * 4 + flip(x, k)), :]
-        last.append(send(here1, here1, core_peer))
     wait(last)
 
 
@@ -499,34 +526,34 @@
             pl.BlockSpec(memory_space=pltpu.HBM),
             pl.BlockSpec(memory_space=pltpu.HBM),
             pl.BlockSpec(memory_space=pltpu.HBM),
-            pl.BlockSpec(memory_space=pltpu.VMEM),
             pl.BlockSpec(memory_space=pltpu.HBM),
-            pl.BlockSpec(memory_space=pltpu.VMEM),
+            pl.BlockSpec(memory_space=pltpu.HBM),
+            pl.BlockSpec(memory_space=pltpu.HBM),
         ],
         out_specs=[pl.BlockSpec(memory_space=pltpu.VMEM)] * 5,
         scratch_shapes=[
             vmem(CIN, 4, 256), vmem(4, CIN, 256), vmem(2, CIN, 256),
             vmem(8, MID + OWN, 128), vmem(MID, 128), vmem(8, OWN, 128), vmem(8, OWN, 128),
-            vmem(MID, CIN * 64), vmem(2, 8, OWN, 2048), vmem(8, OWN, 128),
+            vmem(MID, CIN * 64), vmem(2, 4, 8, OWN, 512), vmem(MID, 128), vmem(8, OWN, 128),
+            vmem(1, MID), vmem(1, OWN),
             half(8, 512, 256), half(8, 512, 256), half(8, 256, 512), half(8, 128, 128),
             half(8 * CIN, 512), half(8 * MID, 512), half(8 * CIN, 256), half(8, 2 * MID, 128),
             vmem(4 * CIN, 512),
             vmem(CIN * 64, 128), vmem(MID * 64, 128), half(CIN * 64, 256), half(MID * 64, 256),
             half(2 * MID, CIN * 64), half(2 * MID, MID * 64),
-            vmem(MID, CIN * 64), vmem(OWN, MID * 64), vmem(8, 128),
+            vmem(MID, 128), vmem(32, CIN * 64), vmem(32, CIN * 64), vmem(OWN, MID * 64), vmem(8, 128),
             vmem(2, CIN, 256), vmem(2, CIN, 256), vmem(2, CIN, 256),
             vmem(32, 2048), vmem(8, 2048), vmem(8, 128),
             vmem(32, 2048), vmem(8, 2048), vmem(8, 128),
-            vmem(3, 8, 2048), vmem(3, 8, 128),
-            vmem(8, 2048), vmem(8, 128),
-            vmem(3, 8, 512), vmem(3, 8, 512), vmem(3, 8, 128),
+            vmem(15, 8, 512), vmem(3, 8, 128), vmem(8, 128),
+            vmem(3, 8, 512), vmem(3, 8, 128),
             vmem(8, 512), vmem(8, 512), vmem(8, 128),
             vmem(3, 8, 128), vmem(3, 8, 128), vmem(3, 8, 128),
             vmem(8, 128), vmem(8, 128), vmem(8, 128),
             vmem(3, 8, 128), vmem(8, 128), vmem(3, 8, 128),
-            pltpu.SemaphoreType.DMA((4,)),
-            pltpu.SemaphoreType.DMA((96,)),
-            pltpu.SemaphoreType.DMA((96,)),
+            pltpu.SemaphoreType.DMA((6,)),
+            pltpu.SemaphoreType.DMA((128,)),
+            pltpu.SemaphoreType.DMA((128,)),
         ],
         compiler_params=pltpu.CompilerParams(
             collective_id=0, has_side_effects=True, vmem_limit_bytes=60 << 20
@@ -573,7 +600,7 @@
 
 def on_device(volume, cotangent, w_first, b_first, w_second, b_second):
     results = stepped(
-        volume[0], cotangent[0], w_first, b_first[:, None], w_second, b_second[:, None]
+        volume[0], cotangent[0], w_first, b_first[None], w_second, b_second[None]
     )
     out, gw1, gw2, gb1, gb2, gvol = finished(*results)
     return (out[None], gvol[None], gw1, gb1, gw2, gb2)

time: 96.7 us -> 92.2 us (0.953)
  Pallas kernels: 93.7 us -> 91.2 us
  local copies, waits for them, and re-layouts: 2.03 us -> 0 us
    pallas_call x1, Pallas kernels: 91.2 us -> 88.7 us  [stepped(): pl.pallas_call(step_kernel, out_shape=(shape((OWN, 128), F32), shape((MID...]
    broadcast_in_dim x2 -> x0, local copies, waits for them, and re-layouts: 1.38 us -> none  [the longest x1 0.71 us: on_device(): b_first[:, None]]
where the time goes in v3:
time: 92.2 us; the launch traced here: 91.9 us
  Pallas kernels  91.2 us (99%)
    pallas_call x1, Pallas kernels, stepped(): pl.pallas_call(step_kernel, out_shape=(shape((OWN, 128), F32), shape((MID...  88.7 us
    pallas_call x1, Pallas kernels, finished(): pl.pallas_call(finish_kernel, out_shape=(shape((OWN, 128), F32), shape((M...  2.53 us

profile of v3, /device:TPU:1, one launch (start us, length us, event | category | flops | bytes accessed | tf_op | source)
XLA Modules:
  0.0 91.9 jit_solution(15428066445996592304)
XLA Ops:
  0.6 88.7 %stepped.1 = (f32[8,128]{1,0:T(8,128)}, f32[64,2048]{1,0:T(8,128)}, f32[8,4096]{1,0:T(8,128)}, f32[8,128]{1,0:T(8,128)}, f32[32,4,256]{2,1,0:T(4,128)}) custom-call(f32[32,4,256]{2,1,0:T(4,128)} %bitcast.6, f32[8,128]{1,0:T(8,128)} %bitcast.7, f32[64,2048]{1,0:T(8,128)} %w1_in.1, f32[1,64]{1,0:T(1,128)} %bitcast.8, f32[8,4096]{1,0:T(8,128)} %w2_in.1, ...), custom_call_target="tpu_custom_call" | custom-call | tf_op jit(solution)/shard_map/stepped/pallas_call | solution.py:516
  89.3 2.5 %finished.1 = (f32[8,128]{1,0:T(8,128)}, f32[64,2048]{1,0:T(8,128)}, f32[8,4096]{1,0:T(8,128)}, f32[64]{0:T(128)}, f32[8]{0:T(128)}, /*index=5*/f32[32,4,256]{2,1,0:T(4,128)}) custom-call(f32[8,128]{1,0:T(8,128)} %get-tuple-element.17.out, f32[64,2048]{1,0:T(8,128)} %get-tuple-element.18.gw1, f32[8,4096]{1,0:T(8,128)} %get-tuple-element.19.gw2, ...), custom_call_target="tpu_custom_call" | custom-call | tf_op jit(solution)/shard_map/finished/pallas_call | solution.py:584

commit v4 on v3

--- a/solution.py
+++ b/solution.py
@@ -72,18 +72,37 @@
             ).astype(BF16)
 
 
-def columns(rows, pick, grid, channels):
-    half = 4 * channels
+def columns(rows, pick, grid, channels, taps):
+    half = 2 * channels
 
     @pl.loop(0, 8, unroll=UNROLL)
     def _(pair):
         both = dot(rows[...], pick[pair], (1, 0))
         value = both[:half] + both[half:]
-        for i in range(4):
+        for order, i in enumerate(taps):
             for second in range(2):
                 grid[pl.ds(i * 16 + 2 * pair + second, channels, stride=64), :] = value[
-                    i * channels : (i + 1) * channels, second * 128 : (second + 1) * 128
+                    order * channels : (order + 1) * channels, second * 128 : (second + 1) * 128
                 ]
+
+
+def all_columns(rows, pick, grid):
+    lane = lax.broadcasted_iota(jnp.int32, (MID, 128), 1)
+
+    @pl.loop(0, 8, unroll=UNROLL)
+    def _(pair):
+        both = dot(rows[...], pick[pair], (1, 0))
+        value = both[: 2 * MID] + both[2 * MID :]
+        for second in range(2):
+            even = value[:MID, second * 128 : (second + 1) * 128]
+            odd = value[MID:, second * 128 : (second + 1) * 128]
+            at = 2 * pair + second
+            before = jnp.where(lane < 16, 0.0, pltpu.roll(odd, 16, 1))
+            after = jnp.where(lane >= 112, 0.0, pltpu.roll(even, 112, 1))
+            grid[pl.ds(at, MID, stride=64), :] = before
+            grid[pl.ds(16 + at, MID, stride=64), :] = even
+            grid[pl.ds(32 + at, MID, stride=64), :] = odd
+            grid[pl.ds(48 + at, MID, stride=64), :] = after
 
 
 def forward(weights, grid, pair_grid, count, depth):
@@ -214,6 +233,7 @@
 
 def step_kernel(
     vol_in, cot_in, w1_in, b1_in, w2_in, b2_in,
+    to_out, to_w1, to_w2, to_bias, to_vol,
     out, tw1, tw2, tbias, tvol,
     raw, planes, halo, hidden, pre1, pre2, grad2, w1, w2, bias1, bias2, row1, row2,
     pick1, pick2, spread1, fold,
@@ -222,7 +242,7 @@
     grad1, gw1, gw1_own, gw2, gbias, edge_out, edge_in, inner,
     c1, c2, c3, s1, s2, s3, xy1, x3, m3, y2, y3, n1, n2, n3,
     r1, r2, r3, o1, o2, o3, a1, a2, a3,
-    loads, sends, receives,
+    loads, stores, sends, receives,
 ):
     dp, me = lax.axis_index("dp"), lax.axis_index("space")
     core, low, y = dp % 2, (dp // 2) % 8, dp // 16
@@ -266,6 +286,13 @@
         copy.start()
         return copy
 
+    stored = []
+
+    def store(source, target):
+        copy = pltpu.make_async_copy(source, target, stores.at[len(stored)])
+        stored.append(copy)
+        copy.start()
+
     def wait(copies):
         for copy in copies:
             copy.wait()
@@ -319,8 +346,9 @@
     def place(i, part, plane):
         high, low_part = split(plane)
         at = slice(part * 256, (part + 1) * 256)
-        rows1[i * CIN : (i + 1) * CIN, at] = high
-        rows1[4 * CIN + i * CIN : 4 * CIN + (i + 1) * CIN, at] = low_part
+        group, order = (0, i - 1) if i in (1, 2) else (1, i // 3)
+        rows1[group, order * CIN : (order + 1) * CIN, at] = high
+        rows1[group, 2 * CIN + order * CIN : 2 * CIN + (order + 1) * CIN, at] = low_part
 
     for i in range(4):
         for part in range(2):
@@ -330,11 +358,12 @@
     high, low_part = split(w1[...])
     w1s[:MID] = high
     w1s[MID:] = low_part
+    columns(rows1.at[0], pick1, grid1, CIN, (1, 2))
     fill_pick(pick2, 2)
     wait(edges)
     place(0, 0, jnp.where(me > 0, halo[0], 0.0))
     place(3, 1, jnp.where(me < 7, halo[1], 0.0))
-    columns(rows1, pick1, grid1, CIN)
+    columns(rows1.at[1], pick1, grid1, CIN, (0, 3))
     wait(cross_w)
     other, other_bias = w2.at[core, y, partner], bias2.at[partner]
     for peer in x_peers:
@@ -368,25 +397,19 @@
     take_weights(core)
     wait(own)
 
-    lane = lax.broadcasted_iota(jnp.int32, (MID, 128), 1)
-    first = lane < 64
-    zero = jnp.zeros((MID, 128), F32)
-
-    def put(i, m, value):
+    first = lax.broadcasted_iota(jnp.int32, (MID, 128), 1) < 64
+
+    def put(odd, m, value):
         high, low_part = split(value)
         at = slice(m * 128, (m + 1) * 128)
-        rows2[i * MID : (i + 1) * MID, at] = high
-        rows2[4 * MID + i * MID : 4 * MID + (i + 1) * MID, at] = low_part
+        rows2[odd * MID : (odd + 1) * MID, at] = high
+        rows2[2 * MID + odd * MID : 2 * MID + (odd + 1) * MID, at] = low_part
 
     for m in range(4):
         near, next_one = hidden[2 * m, :MID], hidden[2 * m + 1, :MID]
-        before = hidden[2 * m - 1, :MID] if m > 0 else zero
-        after = hidden[2 * m + 2, :MID] if m < 3 else zero
-        put(0, m, jnp.where(first, pltpu.roll(before, 64, 1), near))
-        put(1, m, jnp.where(first, near, pltpu.roll(next_one, 64, 1)))
-        put(2, m, jnp.where(first, pltpu.roll(near, 64, 1), next_one))
-        put(3, m, jnp.where(first, next_one, pltpu.roll(after, 64, 1)))
-    columns(rows2, pick2, grid2, MID)
+        put(0, m, jnp.where(first, near, pltpu.roll(next_one, 64, 1)))
+        put(1, m, jnp.where(first, pltpu.roll(near, 64, 1), next_one))
+    all_columns(rows2, pick2, grid2)
     share.wait()
     take_weights(1 - core)
     total = forward(w2s, grid2, pairs2, MID, MID * 64)
@@ -433,6 +456,7 @@
         copies.append(send(piece, y2.at[k - 1], y_peers[k - 1]))
     column_grad(w1s, grad1[...], grid1, MID, CIN * 64)
     out[...] = smooth(pre2[me])
+    store(out, to_out)
     wait(copies)
     shared = lax.broadcasted_iota(jnp.int32, (8, 128), 1) < MID
     here = lanes(y * 512, 512)
@@ -489,19 +513,31 @@
     back2 = [send(piece2, piece2, peer) for peer in y_peers]
     near = o3[...] + a3[0]
     tbias[...] = jnp.where(shared, near + (a3[1] + a3[2]), near)
+    store(tbias, to_bias)
     wait(back2)
     here2 = tw2.at[:, lanes(core * 2048, 2048)]
-    last = [send(here2, here2, core_peer)]
+    last2 = send(here2, here2, core_peer)
+    store(here2, to_w2.at[:, lanes(core * 2048, 2048)])
+    last = []
     for i in range(4):
         for j in range(4):
             if i or j:
                 back1[i, j].wait()
-        here1 = tw1.at[rows(8, core * 4 + flip(x, i)), :]
-        last.append(send(here1, here1, core_peer))
+        block = rows(8, core * 4 + flip(x, i))
+        last.append(send(tw1.at[block, :], tw1.at[block, :], core_peer))
+        store(tw1.at[block, :], to_w1.at[block, :])
     wait(edges)
     tvol[:, 0, :] = inner[0] + jnp.where(me > 0, edge_in[0], 0.0)
     tvol[:, 3, :] = inner[1] + jnp.where(me < 7, edge_in[1], 0.0)
-    wait(last)
+    store(tvol, to_vol)
+    last2.wait()
+    there = lanes((1 - core) * 2048, 2048)
+    store(tw2.at[:, there], to_w2.at[:, there])
+    for i in range(4):
+        last[i].wait()
+        block = rows(8, (1 - core) * 4 + flip(x, i))
+        store(tw1.at[block, :], to_w1.at[block, :])
+    wait(stored)
 
 
 def stepped(vol, cot, w1, b1, w2, b2):
@@ -530,14 +566,15 @@
             pl.BlockSpec(memory_space=pltpu.HBM),
             pl.BlockSpec(memory_space=pltpu.HBM),
         ],
-        out_specs=[pl.BlockSpec(memory_space=pltpu.VMEM)] * 5,
+        out_specs=[pl.BlockSpec(memory_space=pltpu.HBM)] * 5,
         scratch_shapes=[
+            vmem(OWN, 128), vmem(MID, CIN * 64), vmem(OWN, MID * 64), vmem(8, 128), vmem(CIN, 4, 256),
             vmem(CIN, 4, 256), vmem(4, CIN, 256), vmem(2, CIN, 256),
             vmem(8, MID + OWN, 128), vmem(MID, 128), vmem(8, OWN, 128), vmem(8, OWN, 128),
             vmem(MID, CIN * 64), vmem(2, 4, 8, OWN, 512), vmem(MID, 128), vmem(8, OWN, 128),
             vmem(1, MID), vmem(1, OWN),
             half(8, 512, 256), half(8, 512, 256), half(8, 256, 512), half(8, 128, 128),
-            half(8 * CIN, 512), half(8 * MID, 512), half(8 * CIN, 256), half(8, 2 * MID, 128),
+            half(2, 4 * CIN, 512), half(4 * MID, 512), half(8 * CIN, 256), half(8, 2 * MID, 128),
             vmem(4 * CIN, 512),
             vmem(CIN * 64, 128), vmem(MID * 64, 128), half(CIN * 64, 256), half(MID * 64, 256),
             half(2 * MID, CIN * 64), half(2 * MID, MID * 64),
@@ -552,6 +589,7 @@
             vmem(8, 128), vmem(8, 128), vmem(8, 128),
             vmem(3, 8, 128), vmem(8, 128), vmem(3, 8, 128),
             pltpu.SemaphoreType.DMA((6,)),
+            pltpu.SemaphoreType.DMA((16,)),
             pltpu.SemaphoreType.DMA((128,)),
             pltpu.SemaphoreType.DMA((128,)),
         ],
@@ -562,18 +600,33 @@
     )(vol, cot, w1, b1, w2, b2)
 
 
-def finish_kernel(out, gw1, gw2, gbias, gvol, to_out, to_w1, to_w2, to_b1, to_b2, to_vol, done):
-    copies = [
-        pltpu.make_async_copy(source, target, done.at[at])
-        for at, (source, target) in enumerate(
-            [(gw1, to_w1), (gw2, to_w2), (gvol, to_vol), (out, to_out)]
-        )
+def finish_kernel(
+    out, gw1, gw2, gbias, gvol, to_out, to_w1, to_w2, to_b1, to_b2, to_vol,
+    out_here, w1_here, w2_here, bias_here, vol_here, done,
+):
+    through = [
+        (gbias, bias_here, None),
+        (gw1, w1_here, to_w1),
+        (gw2, w2_here, to_w2),
+        (gvol, vol_here, to_vol),
+        (out, out_here, to_out),
     ]
-    for copy in copies:
+    taken = [
+        pltpu.make_async_copy(source, here, done.at[at])
+        for at, (source, here, _) in enumerate(through)
+    ]
+    for copy in taken:
         copy.start()
-    to_b1[...] = gbias[0, :MID]
-    to_b2[...] = gbias[0, MID : MID + OWN]
-    for copy in copies:
+    given = []
+    for at, (_, here, target) in enumerate(through):
+        taken[at].wait()
+        if target is None:
+            to_b1[...] = here[0, :MID]
+            to_b2[...] = here[0, MID : MID + OWN]
+        else:
+            given.append(pltpu.make_async_copy(here, target, done.at[5 + at]))
+            given[-1].start()
+    for copy in given:
         copy.wait()
 
 
@@ -591,9 +644,17 @@
             shape((OWN,), F32),
             shape((CIN, 4, 256), F32),
         ),
-        in_specs=[vmem] * 5,
+        in_specs=[anywhere] * 5,
         out_specs=[anywhere, anywhere, anywhere, vmem, vmem, anywhere],
-        scratch_shapes=[pltpu.SemaphoreType.DMA((4,))],
+        scratch_shapes=[
+            pltpu.VMEM((OWN, 128), F32),
+            pltpu.VMEM((MID, CIN * 64), F32),
+            pltpu.VMEM((OWN, MID * 64), F32),
+            pltpu.VMEM((8, 128), F32),
+            pltpu.VMEM((CIN, 4, 256), F32),
+            pltpu.SemaphoreType.DMA((10,)),
+        ],
+        compiler_params=pltpu.CompilerParams(vmem_limit_bytes=60 << 20),
         name="finished",
     )(out, gw1, gw2, gbias, gvol)
 

time: 92.2 us -> 91.2 us (0.989)
  no operation moved by 1% of the time
where the time goes in v4:
time: 91.2 us; the launch traced here: 91 us
  Pallas kernels  90.4 us (99%)
    pallas_call x1, Pallas kernels, stepped(): pl.pallas_call(step_kernel, out_shape=(shape((OWN, 128), F32), shape((MID...  87.9 us
    pallas_call x1, Pallas kernels, finished(): pl.pallas_call(finish_kernel, out_shape=(shape((OWN, 128), F32), shape((M...  2.52 us

profile of v4, /device:TPU:1, one launch (start us, length us, event | category | flops | bytes accessed | tf_op | source)
XLA Modules:
  0.0 91.0 jit_solution(11848877162624780725)
XLA Ops:
  0.6 87.9 %stepped.1 = (f32[8,128]{1,0:T(8,128)}, f32[64,2048]{1,0:T(8,128)}, f32[8,4096]{1,0:T(8,128)}, f32[8,128]{1,0:T(8,128)}, f32[32,4,256]{2,1,0:T(4,128)}) custom-call(f32[32,4,256]{2,1,0:T(4,128)} %bitcast.6, f32[8,128]{1,0:T(8,128)} %bitcast.7, f32[64,2048]{1,0:T(8,128)} %w1_in.1, f32[1,64]{1,0:T(1,128)} %bitcast.8, f32[8,4096]{1,0:T(8,128)} %w2_in.1, ...), custom_call_target="tpu_custom_call" | custom-call | tf_op jit(solution)/shard_map/stepped/pallas_call | solution.py:552
  88.5 2.5 %finished.1 = (f32[8,128]{1,0:T(8,128)}, f32[64,2048]{1,0:T(8,128)}, f32[8,4096]{1,0:T(8,128)}, f32[64]{0:T(128)}, f32[8]{0:T(128)}, /*index=5*/f32[32,4,256]{2,1,0:T(4,128)}) custom-call(f32[8,128]{1,0:T(8,128)} %get-tuple-element.17.out, f32[64,2048]{1,0:T(8,128)} %get-tuple-element.18.gw1, f32[8,4096]{1,0:T(8,128)} %get-tuple-element.19.gw2, ...), custom_call_target="tpu_custom_call" | custom-call | tf_op jit(solution)/shard_map/finished/pallas_call | solution.py:637

commit v5 on v4

--- a/solution.py
+++ b/solution.py
@@ -505,15 +505,12 @@
         here1 = tw1.at[own_rows, lanes(at1, 128)]
         here2 = tw2.at[:, lanes(at2, 128)]
         copies += [send(here1, here1, peer), send(here2, here2, peer)]
-    copies += [send(o3, a3.at[k], a_peers[k]) for k in range(3)]
+    far_bias = [send(o3, a3.at[k], a_peers[k]) for k in range(3)]
     wait(copies)
     piece1 = tw1.at[own_rows, lanes(y * 512, 512)]
     piece2 = tw2.at[:, lanes(core * 2048 + y * 512, 512)]
     back1 = {at: send(piece1, piece1, peer) for at, peer in xy_peers.items()}
     back2 = [send(piece2, piece2, peer) for peer in y_peers]
-    near = o3[...] + a3[0]
-    tbias[...] = jnp.where(shared, near + (a3[1] + a3[2]), near)
-    store(tbias, to_bias)
     wait(back2)
     here2 = tw2.at[:, lanes(core * 2048, 2048)]
     last2 = send(here2, here2, core_peer)
@@ -526,6 +523,10 @@
         block = rows(8, core * 4 + flip(x, i))
         last.append(send(tw1.at[block, :], tw1.at[block, :], core_peer))
         store(tw1.at[block, :], to_w1.at[block, :])
+    wait(far_bias)
+    near = o3[...] + a3[0]
+    tbias[...] = jnp.where(shared, near + (a3[1] + a3[2]), near)
+    store(tbias, to_bias)
     wait(edges)
     tvol[:, 0, :] = inner[0] + jnp.where(me > 0, edge_in[0], 0.0)
     tvol[:, 3, :] = inner[1] + jnp.where(me < 7, edge_in[1], 0.0)

time: 91.2 us -> 88.7 us (0.973)
  Pallas kernels: 90.4 us -> 87.9 us
    pallas_call x1, Pallas kernels: 87.9 us -> 85.3 us  [stepped(): pl.pallas_call(step_kernel, out_shape=(shape((OWN, 128), F32), shape((MID...]
where the time goes in v5:
time: 88.7 us; the launch traced here: 88.5 us
  Pallas kernels  87.9 us (99%)
    pallas_call x1, Pallas kernels, stepped(): pl.pallas_call(step_kernel, out_shape=(shape((OWN, 128), F32), shape((MID...  85.3 us
    pallas_call x1, Pallas kernels, finished(): pl.pallas_call(finish_kernel, out_shape=(shape((OWN, 128), F32), shape((M...  2.52 us

profile of v5, /device:TPU:1, one launch (start us, length us, event | category | flops | bytes accessed | tf_op | source)
XLA Modules:
  0.0 88.5 jit_solution(4976836222605919524)
XLA Ops:
  0.6 85.3 %stepped.1 = (f32[8,128]{1,0:T(8,128)}, f32[64,2048]{1,0:T(8,128)}, f32[8,4096]{1,0:T(8,128)}, f32[8,128]{1,0:T(8,128)}, f32[32,4,256]{2,1,0:T(4,128)}) custom-call(f32[32,4,256]{2,1,0:T(4,128)} %bitcast.6, f32[8,128]{1,0:T(8,128)} %bitcast.7, f32[64,2048]{1,0:T(8,128)} %w1_in.1, f32[1,64]{1,0:T(1,128)} %bitcast.8, f32[8,4096]{1,0:T(8,128)} %w2_in.1, ...), custom_call_target="tpu_custom_call" | custom-call | tf_op jit(solution)/shard_map/stepped/pallas_call | solution.py:553
  86.0 2.5 %finished.1 = (f32[8,128]{1,0:T(8,128)}, f32[64,2048]{1,0:T(8,128)}, f32[8,4096]{1,0:T(8,128)}, f32[64]{0:T(128)}, f32[8]{0:T(128)}, /*index=5*/f32[32,4,256]{2,1,0:T(4,128)}) custom-call(f32[8,128]{1,0:T(8,128)} %get-tuple-element.17.out, f32[64,2048]{1,0:T(8,128)} %get-tuple-element.18.gw1, f32[8,4096]{1,0:T(8,128)} %get-tuple-element.19.gw2, ...), custom_call_target="tpu_custom_call" | custom-call | tf_op jit(solution)/shard_map/finished/pallas_call | solution.py:638
